TPU v7x, 128 devices: a whole 4x4x4 slice. The times are simulated.
128 devices in a mesh: sec: 64 (over y, x_lo, z, core), scan: 2 (over x_hi).
Axes of the slice: x: 4 (x_hi: 2, x_lo: 2; x = x_hi * 2 + x_lo), y: 4, z: 4, core: 2. Of those that a mesh axis runs over, the one named last changes fastest.
Arguments:
- obj_amp: float32 [64, 512, 512], P('sec', 'scan'), may hold values from 0.97 to 1
- obj_phase: float32 [64, 512, 512], P('sec', 'scan'), may hold values from -3.140625 to 3.140625
- forward_waves: bfloat16 [64, 16, 2, 256, 256], P('sec', 'scan'), may hold values from -6 to 6
- exit_adjoint: bfloat16 [16, 2, 256, 256], P('scan'), may hold values from -6 to 6
- offsets: int32 [16, 2], P('scan'), may hold values from 0 to 256
Outputs:
- object_grad: float32 [64, 2, 512, 512], P('sec', None, 'scan')
All inputs are finite; a program needn't handle non-finite values.
Results may differ from a plain program's by a relative error of at most 0.012.
The roundings to bfloat16 on the way count: a program that leaves them out, or rounds other values in their place, can miss the bound.
Values may be sent and summed in bfloat16 or wider, within the bound.
A program may use at most 64 MiB of HBM per device.

v0:
```python
import jax
import jax.numpy as jnp
from jax import lax
from jax.sharding import PartitionSpec as P

SUBSTEPS = 2


damping = 0.0005
turning = 0.011


def shifted(value, axis, steps):
    count = lax.axis_size(axis)
    first, last = (max(0, -steps), min(count, count - steps))
    return lax.ppermute(value, axis, [(source, source + steps) for source in range(first, last)])


def laplacian(field):
    widths = [(0, 0)] * (field.ndim - 2) + [(1, 1), (1, 1)]
    padded = jnp.pad(field, widths)
    beside = (
        padded[..., 2:, 1:-1]
        + padded[..., :-2, 1:-1]
        + padded[..., 1:-1, 2:]
        + padded[..., 1:-1, :-2]
    )
    return beside - 4.0 * field


def back_step(field):
    for substep in range(SUBSTEPS):
        lap_re = laplacian(field[..., 0, :, :])
        lap_im = laplacian(field[..., 1, :, :])
        new_re = field[..., 0, :, :] + damping * lap_re + turning * lap_im
        new_im = field[..., 1, :, :] + damping * lap_im - turning * lap_re
        field = jnp.stack([new_re, new_im], axis=-3)
    return field


def on_device(obj_amp, obj_phase, forward_waves, exit_adjoint, offsets):
    amp_all, phase_all = (
        lax.all_gather(obj_amp, "scan", axis=1, tiled=True),
        lax.all_gather(obj_phase, "scan", axis=1, tiled=True),
    )
    trans_re = (amp_all * jnp.cos(phase_all))[0]
    trans_im = (amp_all * jnp.sin(phase_all))[0]
    per_tick = 1
    sections = lax.axis_size("sec")
    segment_no = lax.axis_index("sec")
    window = exit_adjoint.shape[-1]
    position_count = exit_adjoint.shape[0]
    batch_total = position_count // per_tick
    tick_count = batch_total + sections - 1
    side = trans_re.shape[-1]
    waves = forward_waves[0]
    zero_index = jnp.zeros((), jnp.int32)

    def one_tick(tick, carry):
        arriving, stored = carry
        batch_no = tick - (sections - 1 - segment_no)
        active = jnp.logical_and(batch_no >= 0, batch_no < batch_total)
        slot = jnp.clip(batch_no, 0, batch_total - 1)
        first_row = slot * per_tick
        own_exit = lax.dynamic_slice_in_dim(exit_adjoint, first_row, per_tick, 0)
        adjoint = jnp.where(segment_no == sections - 1, own_exit, arriving).astype(jnp.float32)
        spread = back_step(adjoint)
        previous = lax.dynamic_index_in_dim(stored, slot, 0, keepdims=False)
        kept = jnp.where(active, spread, previous)
        stored = lax.dynamic_update_index_in_dim(stored, kept, slot, 0)
        corners = lax.dynamic_slice_in_dim(offsets, first_row, per_tick, 0)
        row_at = corners[0, 0]
        col_at = corners[0, 1]
        spread_re = spread[0, 0]
        spread_im = spread[0, 1]
        win_re = lax.dynamic_slice(trans_re, (row_at, col_at), (window, window))
        win_im = lax.dynamic_slice(trans_im, (row_at, col_at), (window, window))
        out_re = win_re * spread_re + win_im * spread_im
        out_im = win_re * spread_im - win_im * spread_re
        outgoing = [jnp.stack([out_re, out_im])]
        leaving = jnp.stack(outgoing).astype(jnp.bfloat16)
        arriving = shifted(leaving, "sec", -1)
        return (arriving, stored)

    start_wave = jnp.zeros((per_tick, 2, window, window), jnp.bfloat16)
    start_store = jnp.zeros((batch_total, per_tick, 2, window, window), jnp.float32)
    arriving, stored = lax.fori_loop(0, tick_count, one_tick, (start_wave, start_store))
    spreads = stored.reshape(position_count, 2, window, window)

    def add_position(position, gradient):
        spread = lax.dynamic_index_in_dim(spreads, position, 0, keepdims=False)
        incoming = lax.dynamic_index_in_dim(waves, position, 0, keepdims=False).astype(jnp.float32)
        part_re = incoming[0] * spread[0] + incoming[1] * spread[1]
        part_im = incoming[0] * spread[1] - incoming[1] * spread[0]
        row_at = offsets[position, 0]
        col_at = offsets[position, 1]
        current = lax.dynamic_slice(gradient, (zero_index, row_at, col_at), (2, window, window))
        added = current + jnp.stack([part_re, part_im])
        return lax.dynamic_update_slice(gradient, added, (zero_index, row_at, col_at))

    start_grad = jnp.zeros((2, side, side), jnp.float32)
    gradient = lax.fori_loop(0, position_count, add_position, start_grad)
    reduced = lax.psum_scatter(gradient, "scan", scatter_dimension=1, tiled=True)
    return reduced[None]


def solution(mesh):
    in_specs = (
        P("sec", "scan", None),
        P("sec", "scan", None),
        P("sec", "scan", None, None, None),
        P("scan", None, None, None),
        P("scan", None),
    )
    out_specs = P("sec", None, "scan", None)
    return jax.shard_map(
        on_device, mesh=mesh, in_specs=in_specs, out_specs=out_specs, check_vma=False
    )
```

profile of v0, /device:TPU:0, one launch (start us, length us, event | category | flops | bytes accessed | tf_op | source)
XLA Modules:
  0.0 1475.1 jit_solution(16604344559426506533)
XLA Ops:
  8.1 28.7 %all-gather.3.cloned.1.call-done = f32[1,512,512]{2,1,0:T(8,128)} async-done(((f32[1,256,512]{2,1,0:T(8,128)}), f32[1,512,512]{2,1,0:T(8,128)}) %all-gather.3.cloned.1.call-update) | async-done | bytes 1048592 | tf_op jit(solution)/shard_map/all_gather | solution.py:43
  36.8 26.4 %all-gather.5.cloned.1.call-done = f32[1,512,512]{2,1,0:T(8,128)} async-done(((f32[1,256,512]{2,1,0:T(8,128)}), f32[1,512,512]{2,1,0:T(8,128)}) %all-gather.5.cloned.1.call-update) | async-done | bytes 1048592 | tf_op jit(solution)/shard_map/all_gather | solution.py:44
  70.6 1150.2 %while.30 = (s32[]{:T(128)}, bf16[1,2,256,256]{3,2,1,0:T(8,128)(2,1)S(1)}, f32[8,1,2,256,256]{4,3,2,1,0:T(8,128)}, s32[]{:T(128)}, s32[8,2]{0,1:T(2,128)S(1)}, /...) while((s32[]{:T(128)}, ...), condition=%wide.region_1.2_spmd, body=%wide.region_0.1_spmd.sunk | while | flops 3538958 | bytes 11534696 | solution.py:87
  293.6 6.6 collective-permute-done
  310.1 6.6 collective-permute-done
  326.6 6.6 collective-permute-done
  343.1 6.6 collective-permute-done
  970.5 6.6 collective-permute-done
  987.0 7.5 collective-permute-done
  1004.4 7.5 collective-permute-done
  1021.8 7.5 collective-permute-done
  1039.2 7.5 collective-permute-done
  1056.6 7.5 collective-permute-done
  1074.1 7.5 collective-permute-done
  1091.5 7.5 collective-permute-done
  1108.9 7.4 collective-permute-done
  1126.2 7.5 collective-permute-done
  1143.6 7.4 collective-permute-done
  1161.0 7.5 collective-permute-done
  1178.4 7.5 collective-permute-done
  1195.9 7.5 collective-permute-done
  1213.3 7.5 collective-permute-done
  1221.0 126.3 %while.31 = (s32[]{:T(128)}, f32[2,512,512]{2,1,0:T(8,128)S(1)}, s32[8,2]{0,1:T(2,128)S(1)}, bf16[8,2,256,256]{3,2,1,0:T(8,128)(2,1)}, f32[8,2,256,256]{3,2,1,0:...) while((s32[]{:T(128)}, f32[2,512,512]{2,1,0:T(8,128)S(1)}, s32[8,2]{0,1:T(2,128)S(1)}, ...), condition=%wide.region_3.4_spmd, body=%wide.region_2.3_spmd.sunk | while | flops 786441 | bytes 4980953 | solution.py:102
  1227.8 8.5 dynamic_update_slice.22
  1243.2 6.9 dynamic_update_slice.22
  1256.9 10.3 dynamic_update_slice.22
  1274.0 10.1 dynamic_update_slice.22
  1290.9 8.2 dynamic_update_slice.22
  1305.9 9.8 dynamic_update_slice.22
  1322.5 8.8 dynamic_update_slice.22
  1338.2 9.1 dynamic_update_slice.22
  1348.7 119.9 %reduce-scatter.2.cloned.1.call-done = f32[2,256,512]{2,1,0:T(8,128)} async-done(((f32[2,512,512]{2,1,0:T(8,128)}), f32[2,256,512]{2,1,0:T(8,128)}) %reduce-scatter.2.cloned.1.call-update) | async-done | bytes 1048592 | tf_op jit(solution)/shard_map/reduce_scatter | solution.py:103
  (879 shorter events, 775.0 us)
Async XLA Ops:
  6.5 30.3 %all-gather.3.cloned.1.call-start = ((), (), s32[]{:S(2)}) async-start(), calls=%async_computation.1 | async-start | bytes 1572864 | tf_op jit(solution)/shard_map/all_gather | solution.py:43
  7.3 56.0 %all-gather.5.cloned.1.call-start = ((), (), s32[]{:S(2)}) async-start(), calls=%async_computation.2 | async-start | bytes 1572864 | tf_op jit(solution)/shard_map/all_gather | solution.py:44
  8.0 1460.6 %reduce-scatter.2.cloned.1.call-start = ((), (), s32[]{:S(2)}) async-start(), calls=%async_computation.3 | async-start | bytes 3145728 | tf_op jit(solution)/shard_map/reduce_scatter | solution.py:103
  290.3 9.8 collective-permute-start
  306.8 9.8 collective-permute-start
  323.4 9.8 collective-permute-start
  339.9 9.8 collective-permute-start
  356.4 9.8 collective-permute-start
  372.9 9.8 collective-permute-start
  389.4 9.8 collective-permute-start
  405.9 9.8 collective-permute-start
  422.4 9.8 collective-permute-start
  438.9 9.8 collective-permute-start
  455.4 9.8 collective-permute-start
  471.9 9.8 collective-permute-start
  488.5 9.8 collective-permute-start
  505.0 9.8 collective-permute-start
  967.2 9.8 collective-permute-start
  983.8 10.7 collective-permute-start
  1001.2 10.7 collective-permute-start
  1018.6 10.7 collective-permute-start
  1036.0 10.7 collective-permute-start
  1053.4 10.7 collective-permute-start
  1070.8 10.7 collective-permute-start
  1088.2 10.7 collective-permute-start
  1105.6 10.6 collective-permute-start
  1123.0 10.7 collective-permute-start
  1140.4 10.7 collective-permute-start
  1157.8 10.7 collective-permute-start
  1175.2 10.8 collective-permute-start
  1192.7 10.7 collective-permute-start
  1210.1 10.7 collective-permute-start
  (44 other events, 380.8 us)
Sparse Core Ops, SparseCore 0:
  9.0 27.7 all-gather.2
  38.5 24.7 all-gather.4
  1348.8 119.7 reduce-scatter.1
where the time goes:
time: 1490 us; the launch traced here: 1480 us
  waiting for transfers between devices  621 us (42%)
  other arithmetic  314 us (21%)
  loops' own time  303 us (20%)
  local copies, waits for them, and re-layouts  132 us (9%)
  starting transfers between devices  91.8 us (6%)
    ppermute x71, waiting for transfers between devices, shifted(): lax.ppermute(value, axis, [(source, source + steps) for source in range(f...  445 us
    another operation x1, loops' own time, on_device(): lax.fori_loop(0, tick_count, one_tick, (start_wave, start_store))  272 us
    dynamic_update_slice x71, other arithmetic, one_tick(): stored = lax.dynamic_update_index_in_dim(stored, kept, slot, 0)  136 us
    reduce_scatter x1, waiting for transfers between devices, on_device(): lax.psum_scatter(gradient, 'scan', scatter_dimension=1, tiled=True)  120 us
    ppermute x71, starting transfers between devices, shifted(): lax.ppermute(value, axis, [(source, source + steps) for source in range(f...  91.7 us
    dynamic_update_slice x8, local copies, waits for them, and re-layouts, add_position(): lax.dynamic_update_slice(gradient, added, (zero_index, row_at, col_at))  71.8 us
    convert_element_type x71, other arithmetic, one_tick(): jnp.where(segment_no == sections - 1, own_exit, arriving)  70.8 us
    another operation x213, other arithmetic, one_tick(): outgoing = [jnp.stack([out_re, out_im])]  44.2 us
  transfers between devices with their start and end apart: 74, of which 74 were waited for; matrix products, arithmetic and copies ran while one was open for 9% of the time, Pallas kernels for 0%

commit v1 on v0

v1 whole, which is shorter than its diff:
```python
import functools

import jax
import jax.numpy as jnp
from jax import lax
from jax.experimental import pallas as pl
from jax.experimental.pallas import tpu as pltpu
from jax.sharding import PartitionSpec as P

MESH = pl.DeviceIdType.MESH

damping = 0.0005
turning = 0.011

G = 8
R = 16
SKEW = 2 * G
W = 256
OBJ = 512
S = (W + SKEW) // R
TOP = 16
ROWS = OBJ + 40
COLS = OBJ + 128
FIX = 32767.0
HELD = jnp.int16


def extract_kernel(offs_ref, trans_ref, win_ref, padded):
    order = G - 1 - lax.rem(lax.axis_index("sec"), G)
    delay = 2 * (order + 1)
    padded[...] = jnp.zeros_like(padded)
    padded[:, TOP : TOP + OBJ, 0:OBJ] = trans_ref[...]

    def per_strip(strip, unused):
        at = lax.broadcasted_iota(jnp.int32, (R, W), 0) + (strip * R - delay)
        inside = jnp.logical_and(at >= 0, at < W)
        for position in range(G):
            row_at = offs_ref[position, 0]
            col_at = offs_ref[position, 1]
            base = pl.multiple_of(col_at // 128 * 128, 128)
            turn = lax.rem(384 - lax.rem(col_at, 128), 384)
            top_row = row_at + (strip * R - delay + TOP)
            row_base = pl.multiple_of(top_row // 8 * 8, 8)
            row_turn = lax.rem(R + 8 - lax.rem(top_row, 8), R + 8)
            for part in range(2):
                rows = padded[part, pl.ds(row_base, R + 8), pl.ds(base, 384)]
                rows = pltpu.roll(rows, row_turn, 0)[0:R]
                rows = pltpu.roll(rows, turn, 1)[:, 0:W]
                rows = jnp.where(inside, rows, 0.0) * FIX
                rows = jnp.where(rows >= 0.0, rows + 0.5, rows - 0.5)
                win_ref[position, strip, part] = rows.astype(jnp.int32).astype(HELD)
        return unused

    lax.fori_loop(0, S, per_strip, 0)


def extract(offsets, trans):
    return pl.pallas_call(
        extract_kernel,
        out_shape=jax.ShapeDtypeStruct((G, S, 2, R, W), HELD),
        in_specs=[
            pl.BlockSpec(memory_space=pltpu.SMEM),
            pl.BlockSpec(memory_space=pltpu.VMEM),
        ],
        out_specs=pl.BlockSpec(memory_space=pltpu.VMEM),
        scratch_shapes=[pltpu.VMEM((2, ROWS, COLS), jnp.float32)],
        name="extract",
    )(offsets, trans)


def laplace(low, mid, high, first, last):
    left = jnp.where(first, 0.0, pltpu.roll(mid, 1, 1))
    right = jnp.where(last, 0.0, pltpu.roll(mid, W - 1, 1))
    return (low + high) + (left + right) - 4.0 * mid


def substep(buf, order, first, last):
    mid_re = buf[order, 0, 7 : 7 + R, :]
    mid_im = buf[order, 1, 7 : 7 + R, :]
    lap_re = laplace(buf[order, 0, 6 : 6 + R, :], mid_re, buf[order, 0, 8 : 8 + R, :], first, last)
    lap_im = laplace(buf[order, 1, 6 : 6 + R, :], mid_im, buf[order, 1, 8 : 8 + R, :], first, last)
    new_re = mid_re + damping * lap_re + turning * lap_im
    new_im = mid_im + damping * lap_im - turning * lap_re
    return new_re, new_im


def sweep_kernel(
    win_ref, exit_ref, spr_ref, trans, inbox, spread_out, wave_out, waves, halves,
    trans_sem, in_sem, spr_sem, trans_sent, spr_sent, wave_sent,
):
    sec = lax.axis_index("sec")
    scan = lax.axis_index("scan")
    group = sec // G
    member = lax.rem(sec, G)
    groups = lax.axis_size("sec") // G
    top = group == groups - 1

    def at(g, m):
        return (g * G + m, scan)

    barrier = pltpu.get_barrier_semaphore()
    for step in range(1, G):
        pl.semaphore_signal(barrier, 1, device_id=at(group, lax.rem(member + step, G)), device_id_type=MESH)

    @pl.when(group > 0)
    def _():
        pl.semaphore_signal(barrier, 1, device_id=at(group - 1, member), device_id_type=MESH)

    @pl.when(jnp.logical_not(top))
    def _():
        pl.semaphore_signal(barrier, 1, device_id=at(group + 1, member), device_id_type=MESH)

    waves[...] = jnp.zeros_like(waves)
    halves[...] = jnp.zeros_like(halves)
    inbox[S - 1] = jnp.zeros((2, R, W), jnp.bfloat16)
    pl.semaphore_wait(barrier, G - 1 + jnp.where(group > 0, 1, 0) + jnp.where(top, 0, 1))

    def give(strip, unused):
        pltpu.make_async_copy(
            win_ref.at[member, strip], trans.at[strip, G - 1 - member], trans_sem.at[strip]
        ).start()
        for step in range(1, G):
            other = lax.rem(member + step, G)
            pltpu.make_async_remote_copy(
                src_ref=win_ref.at[other, strip],
                dst_ref=trans.at[strip, G - 1 - member],
                send_sem=trans_sent,
                recv_sem=trans_sem.at[strip],
                device_id=at(group, other),
                device_id_type=MESH,
            ).start()
        return unused

    lax.fori_loop(0, S, give, 0)

    @pl.when(top)
    def _():
        def feed(strip, unused):
            pltpu.make_async_copy(exit_ref.at[strip], inbox.at[strip], in_sem.at[strip]).start()
            return unused

        lax.fori_loop(0, S - 1, feed, 0)

    lane = lax.broadcasted_iota(jnp.int32, (R, W), 1)
    first = lane == 0
    last = lane == W - 1
    row = lax.broadcasted_iota(jnp.int32, (R, W), 0)

    def one_strip(strip, unused):
        @pl.when(strip < S - 1)
        def _():
            pltpu.make_async_copy(inbox.at[strip], inbox.at[strip], in_sem.at[strip]).wait()

        pltpu.make_async_copy(trans.at[strip], trans.at[strip], trans_sem.at[strip]).wait()
        wave_re = inbox[strip, 0].astype(jnp.float32)
        wave_im = inbox[strip, 1].astype(jnp.float32)
        for order in range(G):
            waves[order, 0, 8 : 8 + R, :] = wave_re
            waves[order, 1, 8 : 8 + R, :] = wave_im
            half_re, half_im = substep(waves, order, first, last)
            at_row = row + (strip * R - 2 * order - 1)
            inside = jnp.logical_and(at_row >= 0, at_row < W)
            halves[order, 0, 8 : 8 + R, :] = jnp.where(inside, half_re, 0.0)
            halves[order, 1, 8 : 8 + R, :] = jnp.where(inside, half_im, 0.0)
            spread_re, spread_im = substep(halves, order, first, last)
            waves[order, :, 0:8, :] = waves[order, :, R : R + 8, :]
            halves[order, :, 0:8, :] = halves[order, :, R : R + 8, :]
            spread_out[strip, order, 0] = spread_re.astype(jnp.bfloat16)
            spread_out[strip, order, 1] = spread_im.astype(jnp.bfloat16)
            win_re = trans[strip, order, 0].astype(jnp.int32).astype(jnp.float32)
            win_im = trans[strip, order, 1].astype(jnp.int32).astype(jnp.float32)
            out_re = ((win_re * spread_re + win_im * spread_im) * (1.0 / FIX)).astype(jnp.bfloat16)
            out_im = ((win_re * spread_im - win_im * spread_re) * (1.0 / FIX)).astype(jnp.bfloat16)
            owner = G - 1 - order

            @pl.when(owner == member)
            def _():
                pltpu.make_async_copy(
                    spread_out.at[strip, order], spr_ref.at[member, strip], spr_sem
                ).start()

            @pl.when(owner != member)
            def _():
                pltpu.make_async_remote_copy(
                    src_ref=spread_out.at[strip, order],
                    dst_ref=spr_ref.at[member, strip],
                    send_sem=spr_sent,
                    recv_sem=spr_sem,
                    device_id=at(group, owner),
                    device_id_type=MESH,
                ).start()

            if order < G - 1:
                wave_re = out_re.astype(jnp.float32)
                wave_im = out_im.astype(jnp.float32)
            else:
                wave_out[strip, 0] = out_re
                wave_out[strip, 1] = out_im

        @pl.when(jnp.logical_and(strip > 0, group > 0))
        def _():
            pltpu.make_async_remote_copy(
                src_ref=wave_out.at[strip],
                dst_ref=inbox.at[strip - 1],
                send_sem=wave_sent,
                recv_sem=in_sem.at[strip - 1],
                device_id=at(group - 1, member),
                device_id_type=MESH,
            ).start()

        return unused

    lax.fori_loop(0, S, one_strip, 0)
    pltpu.make_async_copy(win_ref.at[0 : G - 1], win_ref.at[0 : G - 1], trans_sent).wait()
    pltpu.make_async_copy(spr_ref.at[0 : G - 1], spr_ref.at[0 : G - 1], spr_sent).wait()

    @pl.when(group > 0)
    def _():
        pltpu.make_async_copy(wave_out.at[0 : S - 1], wave_out.at[0 : S - 1], wave_sent).wait()

    pltpu.make_async_copy(spr_ref, spr_ref, spr_sem).wait()


def sweep(win, exit_wave):
    return pl.pallas_call(
        sweep_kernel,
        out_shape=jax.ShapeDtypeStruct((G, S, 2, R, W), jnp.bfloat16),
        in_specs=[pl.BlockSpec(memory_space=pltpu.VMEM)] * 2,
        out_specs=pl.BlockSpec(memory_space=pltpu.VMEM),
        scratch_shapes=[
            pltpu.VMEM((S, G, 2, R, W), HELD),
            pltpu.VMEM((S, 2, R, W), jnp.bfloat16),
            pltpu.VMEM((S, G, 2, R, W), jnp.bfloat16),
            pltpu.VMEM((S, 2, R, W), jnp.bfloat16),
            pltpu.VMEM((G, 2, R + 8, W), jnp.float32),
            pltpu.VMEM((G, 2, R + 8, W), jnp.float32),
            pltpu.SemaphoreType.DMA((S,)),
            pltpu.SemaphoreType.DMA((S,)),
            pltpu.SemaphoreType.DMA,
            pltpu.SemaphoreType.DMA,
            pltpu.SemaphoreType.DMA,
            pltpu.SemaphoreType.DMA,
        ],
        compiler_params=pltpu.CompilerParams(collective_id=0, has_side_effects=True),
        name="sweep",
    )(win, exit_wave)


def gather_kernel(offs_ref, waves_ref, spr_ref, grad_ref, acc):
    order = G - 1 - lax.rem(lax.axis_index("sec"), G)
    delay = 2 * (order + 1)
    acc[...] = jnp.zeros_like(acc)

    for position in range(G):
        row_at = offs_ref[position, 0]
        col_at = offs_ref[position, 1]
        base = pl.multiple_of(col_at // 128 * 128, 128)
        turn = lax.rem(col_at, 128)

        def per_strip(strip, unused):
            fwd_re = waves_ref[position, strip, 0].astype(jnp.float32)
            fwd_im = waves_ref[position, strip, 1].astype(jnp.float32)
            spread_re = spr_ref[position, strip, 0].astype(jnp.float32)
            spread_im = spr_ref[position, strip, 1].astype(jnp.float32)
            at = lax.broadcasted_iota(jnp.int32, (R, W), 0) + (strip * R - delay)
            inside = jnp.logical_and(at >= 0, at < W)
            part_re = jnp.where(inside, fwd_re * spread_re + fwd_im * spread_im, 0.0)
            part_im = jnp.where(inside, fwd_re * spread_im - fwd_im * spread_re, 0.0)
            beside = jnp.zeros((R, 128), jnp.float32)
            below = jnp.zeros((8, 384), jnp.float32)
            top_row = row_at + (strip * R - delay + TOP)
            rows = pl.ds(pl.multiple_of(top_row // 8 * 8, 8), R + 8)
            row_turn = lax.rem(top_row, 8)
            for part, value in enumerate((part_re, part_im)):
                wide = pltpu.roll(jnp.concatenate([value, beside], axis=1), turn, 1)
                tall = pltpu.roll(jnp.concatenate([wide, below], axis=0), row_turn, 0)
                acc[part, rows, pl.ds(base, 384)] += tall
            return unused

        lax.fori_loop(0, S, per_strip, 0)

    grad_ref[...] = acc[:, TOP : TOP + OBJ, 0:OBJ]


def gather(offsets, waves, spread):
    return pl.pallas_call(
        gather_kernel,
        out_shape=jax.ShapeDtypeStruct((2, OBJ, OBJ), jnp.float32),
        in_specs=[
            pl.BlockSpec(memory_space=pltpu.SMEM),
            pl.BlockSpec(memory_space=pltpu.VMEM),
            pl.BlockSpec(memory_space=pltpu.VMEM),
        ],
        out_specs=pl.BlockSpec(memory_space=pltpu.VMEM),
        scratch_shapes=[pltpu.VMEM((2, ROWS, COLS), jnp.float32)],
        name="gather",
    )(offsets, waves, spread)


def on_device(obj_amp, obj_phase, forward_waves, exit_adjoint, offsets):
    trans = jnp.concatenate([obj_amp * jnp.cos(obj_phase), obj_amp * jnp.sin(obj_phase)])
    trans = lax.all_gather(trans, "scan", axis=1, tiled=True)
    win = extract(offsets, trans)
    member = lax.rem(lax.axis_index("sec"), G)
    own = lax.dynamic_index_in_dim(exit_adjoint, member, 0, keepdims=False)
    own = jnp.transpose(own.reshape(2, W // R, R, W), (1, 0, 2, 3))
    spread = sweep(win, own)
    delay = 2 * (G - member)
    waves = jnp.pad(forward_waves[0], ((0, 0), (0, 0), (SKEW, SKEW), (0, 0)))
    waves = lax.dynamic_slice_in_dim(waves, SKEW - delay, W + SKEW, 2)
    waves = jnp.transpose(waves.reshape(G, 2, S, R, W), (0, 2, 1, 3, 4))
    gradient = gather(offsets, waves, spread)
    reduced = lax.psum_scatter(gradient, "scan", scatter_dimension=1, tiled=True)
    return reduced[None]


def solution(mesh):
    in_specs = (
        P("sec", "scan", None),
        P("sec", "scan", None),
        P("sec", "scan", None, None, None),
        P("scan", None, None, None),
        P("scan", None),
    )
    out_specs = P("sec", None, "scan", None)
    return jax.shard_map(
        on_device, mesh=mesh, in_specs=in_specs, out_specs=out_specs, check_vma=False
    )
```

time: 1490 us -> 207 us (0.14)
  waiting for transfers between devices: 621 us -> 65.3 us
  other arithmetic: 314 us -> 4.11 us
  loops' own time: 303 us -> 0 us
  local copies, waits for them, and re-layouts: 132 us -> 5.8 us
  Pallas kernels: 0 us -> 118 us
  starting transfers between devices: 91.8 us -> 0.04 us
    ppermute x71 -> x0, waiting for transfers between devices: 445 us -> none  [shifted(): lax.ppermute(value, axis, [(source, source + steps) for source in range(f...]
    another operation x2 -> x0, loops' own time: 303 us -> none  [the longest x1 272 us: on_device(): lax.fori_loop(0, tick_count, one_tick, (start_wave, start_store))]
    dynamic_update_slice x71 -> x0, other arithmetic: 136 us -> none  [one_tick(): stored = lax.dynamic_update_index_in_dim(stored, kept, slot, 0)]
    pallas_call x0 -> x3, Pallas kernels: none -> 118 us  [the longest x1 93.2 us: sweep(): pl.pallas_call(sweep_kernel, out_shape=jax.ShapeDtypeStruct((G, S, 2, R,...]
    ppermute x71 -> x0, starting transfers between devices: 91.7 us -> none  [shifted(): lax.ppermute(value, axis, [(source, source + steps) for source in range(f...]
    reduce_scatter x1, waiting for transfers between devices: 120 us -> 31.4 us  [on_device(): lax.psum_scatter(gradient, 'scan', scatter_dimension=1, tiled=True)]
    convert_element_type x79 -> x0, other arithmetic: 78.7 us -> none  [the longest x71 70.8 us: one_tick(): jnp.where(segment_no == sections - 1, own_exit, arriving)]
    dynamic_update_slice x8 -> x0, local copies, waits for them, and re-layouts: 71.8 us -> none  [add_position(): lax.dynamic_update_slice(gradient, added, (zero_index, row_at, col_at))]
  transfers between devices with their start and end apart: 74 -> 2, of which waited for: 74 -> 2; matrix products, arithmetic and copies ran while one was open for 9% -> 3% of each run, Pallas kernels for 0% -> 0%
where the time goes in v1:
time: 207 us; the launch traced here: 206 us
  Pallas kernels  118 us (57%)
  waiting for transfers between devices  65.3 us (32%)
  between operations  13.4 us (6%)
  local copies, waits for them, and re-layouts  5.8 us (3%)
  other arithmetic  4.11 us (2%)
    pallas_call x1, Pallas kernels, sweep(): pl.pallas_call(sweep_kernel, out_shape=jax.ShapeDtypeStruct((G, S, 2, R,...  93.2 us
    all_gather x1, waiting for transfers between devices, on_device(): trans = lax.all_gather(trans, 'scan', axis=1, tiled=True)  33.9 us
    reduce_scatter x1, waiting for transfers between devices, on_device(): lax.psum_scatter(gradient, 'scan', scatter_dimension=1, tiled=True)  31.4 us
    pallas_call x1, Pallas kernels, gather(): pl.pallas_call(gather_kernel, out_shape=jax.ShapeDtypeStruct((2, OBJ, OBJ...  17 us
    pallas_call x1, Pallas kernels, extract(): pl.pallas_call(extract_kernel, out_shape=jax.ShapeDtypeStruct((G, S, 2, R...  7.43 us
  transfers between devices with their start and end apart: 2, of which 2 were waited for; matrix products, arithmetic and copies ran while one was open for 3% of the time, Pallas kernels for 0%

profile of v1, /device:TPU:0, one launch (start us, length us, event | category | flops | bytes accessed | tf_op | source)
XLA Modules:
  0.0 206.3 jit_solution(14788168670440946032)
XLA Ops:
  6.5 0.0 copy-start
  6.5 0.0 copy-start.1
  6.5 0.0 all-gather.2.cloned.1.call-start
  6.5 3.1 %cosine_multiply_fusion = (f32[1,256,512]{2,1,0:T(8,128)S(1)}, f32[1,256,512]{2,1,0:T(8,128)S(1)}) fusion(f32[1,256,512]{2,1,0:T(8,128)} %param.5, f32[1,256,512]{2,1,0:T(8,128)} %param.6), kind=kLoop, calls=%fused_computation.4 | loop fusion | flops 262144 | bytes 2097152 | tf_op jit(solution)/shard_map/mul | solution.py:301
  9.6 1.0 pad_maximum_fusion
  10.7 0.0 all-gather.2.cloned.1.call-update
  10.7 0.0 reduce-scatter.2.cloned.1.call-start
  10.7 0.0 copy-done.1
  10.8 0.7 copy.11.offs_ref
  11.4 0.0 copy-done
  11.5 0.7 copy.15
  12.2 2.7 %pad_dynamic-slice_fusion = bf16[8,2,272,256]{3,2,1,0:T(8,128)(2,1)S(1)} fusion(s32[]{:T(128)S(6)} %select_n.7, bf16[8,2,256,256]{3,2,1,0:T(8,128)(2,1)} %bitcast.12), kind=kLoop, calls=%fused_computation | loop fusion | bytes 4325380 | tf_op jit(solution)/shard_map/dynamic_slice | solution.py:310
  14.9 1.7 copy.14
  16.6 33.9 %all-gather.2.cloned.1.call-done.trans_ref = f32[2,512,512]{2,1,0:T(8,128)} async-done(((f32[2,256,512]{2,1,0:T(8,128)}), f32[2,512,512]{2,1,0:T(8,128)}) %all-gather.2.cloned.1.call-update) | async-done | bytes 2097168 | tf_op jit(solution)/shard_map/all_gather | solution.py:302
  50.4 7.4 %extract.1.win_ref = s16[8,17,2,16,256]{4,3,2,1,0:T(8,128)(2,1)} custom-call(s32[8,2]{1,0:T(8,128)} %copy.11.offs_ref, f32[2,512,512]{2,1,0:T(8,128)} %all-gather.2.cloned.1.call-done.trans_ref), custom_call_target="tpu_custom_call" | custom-call | tf_op jit(solution)/shard_map/extract/pallas_call | solution.py:58
  57.9 93.2 %sweep.1.spr_ref = bf16[8,17,2,16,256]{4,3,2,1,0:T(8,128)(2,1)} custom-call(s16[8,17,2,16,256]{4,3,2,1,0:T(8,128)(2,1)} %extract.1.win_ref, bf16[16,2,16,256]{3,2,1,0:T(8,128)(2,1)} %bitcast.13), custom_call_target="tpu_custom_call" | custom-call | tf_op jit(solution)/shard_map/sweep/pallas_call | solution.py:225
  151.1 17.0 %gather.1 = f32[2,512,512]{2,1,0:T(8,128)} custom-call(s32[8,2]{1,0:T(8,128)} %copy.11.offs_ref, bf16[8,17,2,16,256]{4,3,2,1,0:T(8,128)(2,1)} %bitcast.10, bf16[8,17,2,16,256]{4,3,2,1,0:T(8,128)(2,1)} %sweep.1.spr_ref), custom_call_target="tpu_custom_call" | custom-call | tf_op jit(solution)/shard_map/gather/pallas_call | solution.py:286
  168.1 0.0 reduce-scatter.2.cloned.1.call-update
  168.1 31.4 %reduce-scatter.2.cloned.1.call-done = f32[2,256,512]{2,1,0:T(8,128)} async-done(((f32[2,512,512]{2,1,0:T(8,128)}), f32[2,256,512]{2,1,0:T(8,128)}) %reduce-scatter.2.cloned.1.call-update) | async-done | bytes 1048592 | tf_op jit(solution)/shard_map/reduce_scatter | solution.py:313
  (1 shorter events, 0.0 us)
Async XLA Ops:
  6.5 4.9 %copy-start = (bf16[8,2,256,256]{3,2,1,0:T(8,128)(2,1)S(1)}, bf16[8,2,256,256]{3,2,1,0:T(8,128)(2,1)}, u32[]{:S(2)}) copy-start(bf16[8,2,256,256]{3,2,1,0:T(8,128)(2,1)} %param.8) | copy-start | bytes 6291460
  6.5 4.2 %copy-start.1 = (s32[8,2]{0,1:T(2,128)S(1)}, s32[8,2]{0,1:T(2,128)}, u32[]{:S(2)}) copy-start(s32[8,2]{0,1:T(2,128)} %param.9) | copy-start | bytes 196
  6.5 43.9 %all-gather.2.cloned.1.call-start = ((), (), s32[]{:S(2)}) async-start(), calls=%async_computation.1 | async-start | bytes 3145728 | tf_op jit(solution)/shard_map/all_gather | solution.py:302
  10.7 188.8 %reduce-scatter.2.cloned.1.call-start = ((), (), s32[]{:S(2)}) async-start(), calls=%async_computation.2 | async-start | bytes 3145728 | tf_op jit(solution)/shard_map/reduce_scatter | solution.py:313
Sparse Core Ops, SparseCore 0:
  10.8 39.5 all-gather.1
  168.2 31.2 reduce-scatter.1

commit v2 on v1

v2 whole, which is shorter than its diff:
```python
import functools

import jax
import jax.numpy as jnp
from jax import lax
from jax.experimental import pallas as pl
from jax.experimental.pallas import tpu as pltpu
from jax.sharding import PartitionSpec as P

MESH = pl.DeviceIdType.MESH

damping = 0.0005
turning = 0.011

G = 8
R = 16
SKEW = 2 * G
W = 256
OBJ = 512
S = (W + SKEW) // R
TOP = 16
ROWS = OBJ + 40
LATE = 5
COLS = OBJ + 128
FIX = 32767.0
HELD = jnp.int16
BLOCK = 32
BLOCKS = OBJ // 2 // BLOCK


def swap_kernel(half_ref, other_ref, sent, come):
    partner = (lax.axis_index("sec"), 1 - lax.axis_index("scan"))
    barrier = pltpu.get_barrier_semaphore()
    pl.semaphore_signal(barrier, 1, device_id=partner, device_id_type=MESH)
    pl.semaphore_wait(barrier, 1)
    copy = pltpu.make_async_remote_copy(
        src_ref=half_ref, dst_ref=other_ref, send_sem=sent, recv_sem=come, device_id=partner, device_id_type=MESH
    )
    copy.start()
    copy.wait()


def swap(half):
    return pl.pallas_call(
        swap_kernel,
        out_shape=jax.ShapeDtypeStruct(half.shape, half.dtype),
        in_specs=[pl.BlockSpec(memory_space=pltpu.VMEM)],
        out_specs=pl.BlockSpec(memory_space=pltpu.VMEM),
        scratch_shapes=[pltpu.SemaphoreType.DMA, pltpu.SemaphoreType.DMA],
        compiler_params=pltpu.CompilerParams(collective_id=1, has_side_effects=True),
        name="swap",
    )(half)


def turned(pieces, amount, axis, before):
    length = pieces[0].shape[axis]
    places = lax.broadcasted_iota(jnp.int32, pieces[0].shape, axis)
    if before:
        keep = places < length - amount
        rolled = [pltpu.roll(piece, lax.rem(length - amount, length), axis) for piece in pieces]
        return [jnp.where(keep, rolled[i], rolled[i + 1]) for i in range(len(pieces) - 1)]
    keep = places >= amount
    rolled = [pltpu.roll(piece, amount, axis) for piece in pieces]
    zero = jnp.zeros_like(pieces[0])
    rolled = [zero] + rolled + [zero]
    return [jnp.where(keep, rolled[i + 1], rolled[i]) for i in range(len(pieces) + 1)]


def extract_kernel(offs_ref, half_ref, other_ref, win_ref, padded):
    scan = lax.axis_index("scan")
    order = G - 1 - lax.rem(lax.axis_index("sec"), G)
    delay = 2 * (order + 1)
    padded[:, 0:TOP, :] = jnp.zeros((2, TOP, COLS), jnp.int32)
    padded[:, TOP + OBJ :, :] = jnp.zeros((2, ROWS - TOP - OBJ, COLS), jnp.int32)
    padded[:, :, OBJ:] = jnp.zeros((2, ROWS, COLS - OBJ), jnp.int32)

    def place(source, start):
        def some_rows(block, unused):
            rows = pl.ds(pl.multiple_of(block * 32, 32), 32)
            to = pl.ds(pl.multiple_of(start + block * 32, 8), 32)
            for part in range(2):
                padded[part, to, 0:OBJ] = source[part, rows, :].astype(jnp.int32)
            return unused

        lax.fori_loop(0, OBJ // 64, some_rows, 0)

    place(half_ref, pl.multiple_of(TOP + scan * (OBJ // 2), 8))
    place(other_ref, pl.multiple_of(TOP + (1 - scan) * (OBJ // 2), 8))

    def per_strip(strip, unused):
        at = lax.broadcasted_iota(jnp.int32, (R, 128), 0) + (strip * R - delay)
        inside = jnp.logical_and(at >= 0, at < W)
        for position in range(G):
            row_at = offs_ref[position, 0]
            col_at = offs_ref[position, 1]
            base = pl.multiple_of(col_at // 128 * 128, 128)
            top_row = row_at + (strip * R - delay + TOP)
            row_base = pl.multiple_of(top_row // 8 * 8, 8)
            for part in range(2):
                whole = padded[part, pl.ds(row_base, R + 8), pl.ds(base, 384)]
                tiles = [
                    turned([whole[8 * i : 8 * i + 8, 128 * j : 128 * j + 128] for j in range(3)], lax.rem(col_at, 128), 1, True)
                    for i in range(R // 8 + 1)
                ]
                for j in range(2):
                    column = turned([tile[j] for tile in tiles], lax.rem(top_row, 8), 0, True)
                    column = jnp.where(inside, jnp.concatenate(column, axis=0), 0)
                    win_ref[position, strip, part, :, 128 * j : 128 * j + 128] = column.astype(HELD)
        return unused

    lax.fori_loop(0, S, per_strip, 0)


def extract(offsets, half, other):
    return pl.pallas_call(
        extract_kernel,
        out_shape=jax.ShapeDtypeStruct((G, S, 2, R, W), HELD),
        in_specs=[
            pl.BlockSpec(memory_space=pltpu.SMEM),
            pl.BlockSpec(memory_space=pltpu.VMEM),
            pl.BlockSpec(memory_space=pltpu.VMEM),
        ],
        out_specs=pl.BlockSpec(memory_space=pltpu.VMEM),
        scratch_shapes=[pltpu.VMEM((2, ROWS, COLS), jnp.int32)],
        name="extract",
    )(offsets, half, other)


def laplace(low, mid, high, first, last):
    left = jnp.where(first, 0.0, pltpu.roll(mid, 1, 1))
    right = jnp.where(last, 0.0, pltpu.roll(mid, W - 1, 1))
    return (low + high) + (left + right) - 4.0 * mid


def substep(buf, order, first, last):
    mid_re = buf[order, 0, 7 : 7 + R, :]
    mid_im = buf[order, 1, 7 : 7 + R, :]
    lap_re = laplace(buf[order, 0, 6 : 6 + R, :], mid_re, buf[order, 0, 8 : 8 + R, :], first, last)
    lap_im = laplace(buf[order, 1, 6 : 6 + R, :], mid_im, buf[order, 1, 8 : 8 + R, :], first, last)
    new_re = mid_re + damping * lap_re + turning * lap_im
    new_im = mid_im + damping * lap_im - turning * lap_re
    return new_re, new_im


def sweep_kernel(
    windows, exit_ref, spr_ref, trans, inbox, spread_out, wave_out, waves, halves, tall,
    trans_sem, in_sem, spr_sem, trans_sent, spr_sent, wave_sent,
):
    sec = lax.axis_index("sec")
    scan = lax.axis_index("scan")
    group = sec // G
    member = lax.rem(sec, G)
    groups = lax.axis_size("sec") // G
    top = group == groups - 1

    def at(g, m):
        return (g * G + m, scan)

    barrier = pltpu.get_barrier_semaphore()
    for step in range(1, G):
        pl.semaphore_signal(barrier, 1, device_id=at(group, lax.rem(member + step, G)), device_id_type=MESH)

    @pl.when(group > 0)
    def _():
        pl.semaphore_signal(barrier, 1, device_id=at(group - 1, member), device_id_type=MESH)

    @pl.when(jnp.logical_not(top))
    def _():
        pl.semaphore_signal(barrier, 1, device_id=at(group + 1, member), device_id_type=MESH)

    pl.semaphore_wait(barrier, G - 1 + jnp.where(group > 0, 1, 0) + jnp.where(top, 0, 1))
    waves[...] = jnp.zeros_like(waves)
    halves[...] = jnp.zeros_like(halves)
    tall[...] = jnp.zeros_like(tall)
    inbox[S - 1] = jnp.zeros((2, R, W), jnp.bfloat16)
    @pl.when(top)
    def _():
        def feed(strip, unused):
            inbox[strip] = exit_ref[strip]
            return unused

        lax.fori_loop(0, S - 1, feed, 0)

    mine = G - 1 - member

    def give(strip, unused):
        for step in range(1, G):
            person = lax.rem(member + step, G)
            pltpu.make_async_remote_copy(
                src_ref=windows.at[person, strip],
                dst_ref=trans.at[strip, mine],
                send_sem=trans_sent,
                recv_sem=trans_sem.at[strip],
                device_id=at(group, person),
                device_id_type=MESH,
            ).start()
        return unused

    lax.fori_loop(0, S, give, 0)

    def own(strip, unused):
        trans[strip, mine] = windows[member, strip]
        return unused

    lax.fori_loop(0, S, own, 0)

    lane = lax.broadcasted_iota(jnp.int32, (R, W), 1)
    first = lane == 0
    last = lane == W - 1
    row = lax.broadcasted_iota(jnp.int32, (R, W), 0)

    def send_spread(strip, order):
        pltpu.make_async_remote_copy(
            src_ref=spread_out.at[strip, order],
            dst_ref=spr_ref.at[member, strip],
            send_sem=spr_sent,
            recv_sem=spr_sem,
            device_id=at(group, G - 1 - order),
            device_id_type=MESH,
        ).start()

    def one_strip(strip, unused):
        @pl.when(jnp.logical_and(strip < S - 1, jnp.logical_not(top)))
        def _():
            pltpu.make_async_copy(inbox.at[strip], inbox.at[strip], in_sem.at[strip]).wait()

        pltpu.make_async_copy(
            trans.at[strip, 0 : G - 1], trans.at[strip, 0 : G - 1], trans_sem.at[strip]
        ).wait()
        before = jnp.maximum(strip - 1, 0)
        wave_re = inbox[strip, 0].astype(jnp.float32)
        wave_im = inbox[strip, 1].astype(jnp.float32)
        for order in range(G):
            waves[order, 0, 8 : 8 + R, :] = wave_re
            waves[order, 1, 8 : 8 + R, :] = wave_im
            half_re, half_im = substep(waves, order, first, last)
            at_row = row + (strip * R - 2 * order - 1)
            inside = jnp.logical_and(at_row >= 0, at_row < W)
            halves[order, 0, 8 : 8 + R, :] = jnp.where(inside, half_re, 0.0)
            halves[order, 1, 8 : 8 + R, :] = jnp.where(inside, half_im, 0.0)
            spread_re, spread_im = substep(halves, order, first, last)
            waves[order, :, 0:8, :] = waves[order, :, R : R + 8, :]
            halves[order, :, 0:8, :] = halves[order, :, R : R + 8, :]
            win_re = trans[strip, order, 0].astype(jnp.int32).astype(jnp.float32)
            win_im = trans[strip, order, 1].astype(jnp.int32).astype(jnp.float32)
            out_re = ((win_re * spread_re + win_im * spread_im) * (1.0 / FIX)).astype(jnp.bfloat16)
            out_im = ((win_re * spread_im - win_im * spread_re) * (1.0 / FIX)).astype(jnp.bfloat16)
            lag = 2 * (order + 1)
            tall[order, 0, R : 2 * R, :] = spread_re
            tall[order, 1, R : 2 * R, :] = spread_im
            spread_out[before, order] = tall[order, :, lag : lag + R, :].astype(jnp.bfloat16)
            tall[order, :, 0:R, :] = tall[order, :, R : 2 * R, :]

            @pl.when(jnp.logical_and(strip > 0, jnp.logical_and(group < LATE, member != G - 1 - order)))
            def _():
                send_spread(strip - 1, order)

            if order < G - 1:
                wave_re = out_re.astype(jnp.float32)
                wave_im = out_im.astype(jnp.float32)
            else:
                wave_out[before, 0] = out_re
                wave_out[before, 1] = out_im

        @pl.when(strip > 0)
        def _():
            spr_ref[member, strip - 1] = spread_out[strip - 1, mine]

        @pl.when(jnp.logical_and(strip > 0, group > 0))
        def _():
            pltpu.make_async_remote_copy(
                src_ref=wave_out.at[strip - 1],
                dst_ref=inbox.at[strip - 1],
                send_sem=wave_sent,
                recv_sem=in_sem.at[strip - 1],
                device_id=at(group - 1, member),
                device_id_type=MESH,
            ).start()

        return unused

    lax.fori_loop(0, S, one_strip, 0)

    @pl.when(group >= LATE)
    def _():
        def rest(strip, unused):
            for order in range(G):

                @pl.when(member != G - 1 - order)
                def _():
                    send_spread(strip, order)

            return unused

        lax.fori_loop(0, S - 1, rest, 0)

    pltpu.make_async_copy(windows.at[0 : G - 1], windows.at[0 : G - 1], trans_sent).wait()
    pltpu.make_async_copy(spr_ref.at[0 : G - 1], spr_ref.at[0 : G - 1], spr_sent).wait()

    @pl.when(group > 0)
    def _():
        pltpu.make_async_copy(wave_out, wave_out, wave_sent).wait()

    pltpu.make_async_copy(spr_ref.at[0 : G - 1], spr_ref.at[0 : G - 1], spr_sem).wait()


def sweep(windows, exit_wave):
    return pl.pallas_call(
        sweep_kernel,
        out_shape=jax.ShapeDtypeStruct((G, S - 1, 2, R, W), jnp.bfloat16),
        in_specs=[pl.BlockSpec(memory_space=pltpu.VMEM)] * 2,
        out_specs=pl.BlockSpec(memory_space=pltpu.VMEM),
        scratch_shapes=[
            pltpu.VMEM((S, G, 2, R, W), HELD),
            pltpu.VMEM((S, 2, R, W), jnp.bfloat16),
            pltpu.VMEM((S - 1, G, 2, R, W), jnp.bfloat16),
            pltpu.VMEM((S - 1, 2, R, W), jnp.bfloat16),
            pltpu.VMEM((G, 2, R + 8, W), jnp.float32),
            pltpu.VMEM((G, 2, R + 8, W), jnp.float32),
            pltpu.VMEM((G, 2, 2 * R, W), jnp.float32),
            pltpu.SemaphoreType.DMA((S,)),
            pltpu.SemaphoreType.DMA((S - 1,)),
            pltpu.SemaphoreType.DMA,
            pltpu.SemaphoreType.DMA,
            pltpu.SemaphoreType.DMA,
            pltpu.SemaphoreType.DMA,
        ],
        compiler_params=pltpu.CompilerParams(collective_id=0, has_side_effects=True),
        name="sweep",
    )(windows, exit_wave)


def gather_kernel(offs_ref, fwd_ref, spr_ref, grad_ref, acc):
    acc[...] = jnp.zeros_like(acc)

    def per_position(position, unused):
        row_at = offs_ref[position, 0]
        col_at = offs_ref[position, 1]
        base = pl.multiple_of(col_at // 128 * 128, 128)

        def per_strip(strip, unused):
            rows = pl.ds(pl.multiple_of(strip * R, R), R)
            to = pl.ds(pl.multiple_of((row_at // 8 * 8) + strip * R, 8), R + 8)
            fwd_re = fwd_ref[position, 0, rows, :].astype(jnp.float32)
            fwd_im = fwd_ref[position, 1, rows, :].astype(jnp.float32)
            spread_re = spr_ref[position, strip, 0].astype(jnp.float32)
            spread_im = spr_ref[position, strip, 1].astype(jnp.float32)
            here = (fwd_re * spread_re + fwd_im * spread_im, fwd_re * spread_im - fwd_im * spread_re)
            for part in range(2):
                tiles = [
                    turned(
                        [here[part][8 * i : 8 * i + 8, 128 * j : 128 * j + 128] for j in range(2)],
                        lax.rem(col_at, 128),
                        1,
                        False,
                    )
                    for i in range(R // 8)
                ]
                columns = [
                    jnp.concatenate(turned([tile[j] for tile in tiles], lax.rem(row_at, 8), 0, False), axis=0)
                    for j in range(3)
                ]
                acc[part, to, pl.ds(base, 384)] += jnp.concatenate(columns, axis=1)
            return unused

        lax.fori_loop(0, S - 1, per_strip, 0)
        return unused

    lax.fori_loop(0, G, per_position, 0)
    grad_ref[...] = acc[:, 0:OBJ, 0:OBJ]


def gather(offsets, forward, spread):
    return pl.pallas_call(
        gather_kernel,
        out_shape=jax.ShapeDtypeStruct((2, OBJ, OBJ), jnp.float32),
        in_specs=[
            pl.BlockSpec(memory_space=pltpu.SMEM),
            pl.BlockSpec(memory_space=pltpu.VMEM),
            pl.BlockSpec(memory_space=pltpu.VMEM),
        ],
        out_specs=pl.BlockSpec(memory_space=pltpu.VMEM),
        scratch_shapes=[pltpu.VMEM((2, OBJ + 8, COLS), jnp.float32)],
        name="gather",
    )(offsets, forward, spread)


def reduce_kernel(grad_ref, out_ref, leaving, landing, sent, come):
    scan = lax.axis_index("scan")
    partner = (lax.axis_index("sec"), 1 - scan)
    barrier = pltpu.get_barrier_semaphore()
    pl.semaphore_signal(barrier, 1, device_id=partner, device_id_type=MESH)

    def chunk(block):
        return pltpu.make_async_remote_copy(
            src_ref=leaving.at[block],
            dst_ref=landing.at[block],
            send_sem=sent.at[block],
            recv_sem=come.at[block],
            device_id=partner,
            device_id_type=MESH,
        )

    pl.semaphore_wait(barrier, 1)

    def give(block, unused):
        rows = pl.ds(pl.multiple_of((1 - scan) * (OBJ // 2) + block * BLOCK, BLOCK), BLOCK)
        leaving[block] = grad_ref[:, rows, :].astype(jnp.bfloat16)
        chunk(block).start()
        return unused

    def join(block, unused):
        chunk(block).wait()
        rows = pl.ds(pl.multiple_of(scan * (OBJ // 2) + block * BLOCK, BLOCK), BLOCK)
        to = pl.ds(pl.multiple_of(block * BLOCK, BLOCK), BLOCK)
        out_ref[:, to, :] = grad_ref[:, rows, :] + landing[block].astype(jnp.float32)
        return unused

    lax.fori_loop(0, BLOCKS, give, 0)
    lax.fori_loop(0, BLOCKS, join, 0)


def reduce(gradient):
    return pl.pallas_call(
        reduce_kernel,
        out_shape=jax.ShapeDtypeStruct((2, OBJ // 2, OBJ), jnp.float32),
        in_specs=[pl.BlockSpec(memory_space=pltpu.VMEM)],
        out_specs=pl.BlockSpec(memory_space=pltpu.VMEM),
        scratch_shapes=[
            pltpu.VMEM((BLOCKS, 2, BLOCK, OBJ), jnp.bfloat16),
            pltpu.VMEM((BLOCKS, 2, BLOCK, OBJ), jnp.bfloat16),
            pltpu.SemaphoreType.DMA((BLOCKS,)),
            pltpu.SemaphoreType.DMA((BLOCKS,)),
        ],
        compiler_params=pltpu.CompilerParams(collective_id=2, has_side_effects=True),
        name="reduce",
    )(gradient)


def on_device(obj_amp, obj_phase, forward_waves, exit_adjoint, offsets):
    trans = jnp.concatenate([obj_amp * jnp.cos(obj_phase), obj_amp * jnp.sin(obj_phase)])
    half = jnp.round(trans * FIX).astype(jnp.int32).astype(HELD)
    member = lax.rem(lax.axis_index("sec"), G)
    own = lax.dynamic_index_in_dim(exit_adjoint, member, 0, keepdims=False)
    own = jnp.transpose(own.reshape(2, W // R, R, W), (1, 0, 2, 3))
    spread = sweep(extract(offsets, half, swap(half)), own)
    return reduce(gather(offsets, forward_waves[0], spread))[None]


def solution(mesh):
    in_specs = (
        P("sec", "scan", None),
        P("sec", "scan", None),
        P("sec", "scan", None, None, None),
        P("scan", None, None, None),
        P("scan", None),
    )
    out_specs = P("sec", None, "scan", None)
    return jax.shard_map(
        on_device, mesh=mesh, in_specs=in_specs, out_specs=out_specs, check_vma=False
    )
```

time: 207 us -> 159 us (0.77)
  waiting for transfers between devices: 65.3 us -> 0 us
  Pallas kernels: 118 us -> 150 us
  between operations: 13.4 us -> 0.04 us
    pallas_call x1 -> x3, Pallas kernels: 93.2 us -> 128 us  [the longest x1 93.5 us: sweep(): pl.pallas_call(sweep_kernel, out_shape=jax.ShapeDtypeStruct((G, S - 1, 2,...]
    all_gather x1 -> x0, waiting for transfers between devices: 33.9 us -> none  [on_device(): trans = lax.all_gather(trans, 'scan', axis=1, tiled=True)]
    reduce_scatter x1 -> x0, waiting for transfers between devices: 31.4 us -> none  [on_device(): lax.psum_scatter(gradient, 'scan', scatter_dimension=1, tiled=True)]
    unnamed x5 -> x4, local copies, waits for them, and re-layouts: 0.68 us -> 3.87 us
    dynamic_slice x1 -> x0, local copies, waits for them, and re-layouts: 2.71 us -> none  [on_device(): waves = lax.dynamic_slice_in_dim(waves, SKEW - delay, W + SKEW, 2)]
  transfers between devices with their start and end apart: 2 -> 0, of which waited for: 2 -> 0; matrix products, arithmetic and copies ran while one was open for 3% -> 0% of each run, Pallas kernels for 0% -> 0%
where the time goes in v2:
time: 159 us; the launch traced here: 158 us
  Pallas kernels  150 us (94%)
  local copies, waits for them, and re-layouts  4.61 us (3%)
  other arithmetic  3.83 us (2%)
    pallas_call x1, Pallas kernels, sweep(): pl.pallas_call(sweep_kernel, out_shape=jax.ShapeDtypeStruct((G, S - 1, 2,...  93.5 us
    pallas_call x1, Pallas kernels, reduce(): pl.pallas_call(reduce_kernel, out_shape=jax.ShapeDtypeStruct((2, OBJ // 2...  17.7 us
    pallas_call x1, Pallas kernels, swap(): pl.pallas_call(swap_kernel, out_shape=jax.ShapeDtypeStruct(half.shape, ha...  16.9 us
    pallas_call x1, Pallas kernels, gather(): pl.pallas_call(gather_kernel, out_shape=jax.ShapeDtypeStruct((2, OBJ, OBJ...  14.9 us
    pallas_call x1, Pallas kernels, extract(): pl.pallas_call(extract_kernel, out_shape=jax.ShapeDtypeStruct((G, S, 2, R...  6.81 us
    unnamed x4, local copies, waits for them, and re-layouts  3.87 us

profile of v2, /device:TPU:0, one launch (start us, length us, event | category | flops | bytes accessed | tf_op | source)
XLA Modules:
  0.0 158.4 jit_solution(556411915021806650)
XLA Ops:
  0.0 0.0 copy-start
  0.0 1.5 copy.10.offs_ref
  1.5 0.1 copy-done
  1.6 0.7 copy.12
  2.4 2.9 %cosine_multiply_fusion = (f32[1,256,512]{2,1,0:T(8,128)S(1)}, f32[1,256,512]{2,1,0:T(8,128)S(1)}) fusion(f32[1,256,512]{2,1,0:T(8,128)} %param.5, f32[1,256,512]{2,1,0:T(8,128)} %param.6), kind=kLoop, calls=%fused_computation.5 | loop fusion | flops 262144 | bytes 2097152 | tf_op jit(solution)/shard_map/mul | solution.py:441
  5.3 0.9 fusion.2.half_ref
  6.2 16.9 %swap.1.other_ref = s16[2,256,512]{2,1,0:T(8,128)(2,1)} custom-call(s16[2,256,512]{2,1,0:T(8,128)(2,1)} %fusion.2.half_ref), custom_call_target="tpu_custom_call" | custom-call | tf_op jit(solution)/shard_map/swap/pallas_call | solution.py:44
  23.1 6.8 %extract.1.windows = s16[8,17,2,16,256]{4,3,2,1,0:T(8,128)(2,1)} custom-call(s32[8,2]{1,0:T(8,128)} %copy.10.offs_ref, s16[2,256,512]{2,1,0:T(8,128)(2,1)} %fusion.2.half_ref, s16[2,256,512]{2,1,0:T(8,128)(2,1)} %swap.1.other_ref), custom_call_target="tpu_custom_call" | custom-call | tf_op jit(solution)/shard_map/extract/pallas_call | solution.py:115
  29.9 93.5 %sweep.1.spr_ref = bf16[8,16,2,16,256]{4,3,2,1,0:T(8,128)(2,1)} custom-call(s16[8,17,2,16,256]{4,3,2,1,0:T(8,128)(2,1)} %extract.1.windows, bf16[16,2,16,256]{3,2,1,0:T(8,128)(2,1)} %bitcast.8), custom_call_target="tpu_custom_call" | custom-call | tf_op jit(solution)/shard_map/sweep/pallas_call | solution.py:308
  123.5 14.9 %gather.1.grad_ref = f32[2,512,512]{2,1,0:T(8,128)} custom-call(s32[8,2]{1,0:T(8,128)} %copy.10.offs_ref, bf16[8,2,256,256]{3,2,1,0:T(8,128)(2,1)} %bitcast.7, bf16[8,16,2,16,256]{4,3,2,1,0:T(8,128)(2,1)} %sweep.1.spr_ref), custom_call_target="tpu_custom_call" | custom-call | tf_op jit(solution)/shard_map/gather/pallas_call | solution.py:374
  138.4 17.7 %reduce.1 = f32[2,256,512]{2,1,0:T(8,128)} custom-call(f32[2,512,512]{2,1,0:T(8,128)} %gather.1.grad_ref), custom_call_target="tpu_custom_call" | custom-call | tf_op jit(solution)/shard_map/reduce/pallas_call | solution.py:424
  156.1 2.3 %copy.14 = f32[1,2,256,512]{3,2,1,0:T(8,128)} copy(f32[1,2,256,512]{3,2,1,0:T(8,128)} %bitcast.6) | data formatting | bytes 2097152
  (1 shorter events, 0.0 us)
Async XLA Ops:
  0.0 1.6 %copy-start = (bf16[8,2,256,256]{3,2,1,0:T(8,128)(2,1)S(1)}, bf16[8,2,256,256]{3,2,1,0:T(8,128)(2,1)}, u32[]{:S(2)}) copy-start(bf16[8,2,256,256]{3,2,1,0:T(8,128)(2,1)} %param.8) | copy-start | bytes 6291460

commit v3 on v2

v3 whole, which is shorter than its diff:
```python
import functools

import jax
import jax.numpy as jnp
from jax import lax
from jax.experimental import pallas as pl
from jax.experimental.pallas import tpu as pltpu
from jax.sharding import PartitionSpec as P

MESH = pl.DeviceIdType.MESH

damping = 0.0005
turning = 0.011

G = 8
R = 16
SKEW = 2 * G
W = 256
OBJ = 512
S = (W + SKEW) // R
TOP = 16
ROWS = OBJ + 40
LATE = 5
COLS = OBJ + 128
FIX = 32767.0
HELD = jnp.int16
BLOCK = 32
BLOCKS = OBJ // 2 // BLOCK


def swap_kernel(amp_ref, phase_ref, half_ref, other_ref, sent, come):
    partner = (lax.axis_index("sec"), 1 - lax.axis_index("scan"))
    barrier = pltpu.get_barrier_semaphore()
    pl.semaphore_signal(barrier, 1, device_id=partner, device_id_type=MESH)
    pl.semaphore_wait(barrier, 1)

    def chunk(block):
        rows = pl.ds(pl.multiple_of(block * BLOCK, BLOCK), BLOCK)
        return pltpu.make_async_remote_copy(
            src_ref=half_ref.at[:, rows, :],
            dst_ref=other_ref.at[:, rows, :],
            send_sem=sent.at[block],
            recv_sem=come.at[block],
            device_id=partner,
            device_id_type=MESH,
        )

    def fixed(value):
        value = value * FIX
        return jnp.where(value >= 0.0, value + 0.5, value - 0.5).astype(jnp.int32).astype(HELD)

    def give(block, unused):
        rows = pl.ds(pl.multiple_of(block * BLOCK, BLOCK), BLOCK)
        amp = amp_ref[rows, :]
        phase = phase_ref[rows, :]
        half_ref[0, rows, :] = fixed(amp * jnp.cos(phase))
        half_ref[1, rows, :] = fixed(amp * jnp.sin(phase))
        chunk(block).start()
        return unused

    def take(block, unused):
        chunk(block).wait()
        return unused

    lax.fori_loop(0, BLOCKS, give, 0)
    lax.fori_loop(0, BLOCKS, take, 0)


def swap(amp, phase):
    rows = jax.ShapeDtypeStruct((2, OBJ // 2, OBJ), HELD)
    return pl.pallas_call(
        swap_kernel,
        out_shape=(rows, rows),
        in_specs=[pl.BlockSpec(memory_space=pltpu.VMEM)] * 2,
        out_specs=[pl.BlockSpec(memory_space=pltpu.VMEM)] * 2,
        scratch_shapes=[pltpu.SemaphoreType.DMA((BLOCKS,)), pltpu.SemaphoreType.DMA((BLOCKS,))],
        compiler_params=pltpu.CompilerParams(collective_id=1, has_side_effects=True),
        name="swap",
    )(amp, phase)


def extract_kernel(offs_ref, half_ref, other_ref, win_ref, padded):
    scan = lax.axis_index("scan")
    order = G - 1 - lax.rem(lax.axis_index("sec"), G)
    delay = 2 * (order + 1)

    def place(source, start):
        def some_rows(block, unused):
            rows = pl.ds(pl.multiple_of(block * BLOCK, BLOCK), BLOCK)
            to = pl.ds(pl.multiple_of(start + block * BLOCK, 8), BLOCK)
            for part in range(2):
                for j in range(OBJ // 128):
                    padded[part, j, to, :] = source[part, rows, 128 * j : 128 * j + 128].astype(jnp.int32)
            return unused

        lax.fori_loop(0, BLOCKS, some_rows, 0)

    place(half_ref, pl.multiple_of(TOP + scan * (OBJ // 2), 8))
    place(other_ref, pl.multiple_of(TOP + (1 - scan) * (OBJ // 2), 8))
    lane = lax.broadcasted_iota(jnp.int32, (R, 128), 1)

    def per_strip(strip, unused):
        at = lax.broadcasted_iota(jnp.int32, (R, 128), 0) + (strip * R - delay)
        inside = jnp.logical_and(at >= 0, at < W)
        for position in range(G):
            col_at = offs_ref[position, 1]
            column = col_at // 128
            over = lax.rem(col_at, 128)
            turn = lax.rem(128 - over, 128)
            keep = lane < 128 - over
            rows = pl.ds(offs_ref[position, 0] + (strip * R - delay + TOP), R)
            for part in range(2):
                rolled = [pltpu.roll(padded[part, column + j, rows, :], turn, 1) for j in range(3)]
                for j in range(2):
                    value = jnp.where(inside, jnp.where(keep, rolled[j], rolled[j + 1]), 0)
                    win_ref[position, strip, part, :, 128 * j : 128 * j + 128] = value.astype(HELD)
        return unused

    lax.fori_loop(0, S, per_strip, 0)


def extract(offsets, half, other):
    return pl.pallas_call(
        extract_kernel,
        out_shape=jax.ShapeDtypeStruct((G, S, 2, R, W), HELD),
        in_specs=[
            pl.BlockSpec(memory_space=pltpu.SMEM),
            pl.BlockSpec(memory_space=pltpu.VMEM),
            pl.BlockSpec(memory_space=pltpu.VMEM),
        ],
        out_specs=pl.BlockSpec(memory_space=pltpu.VMEM),
        scratch_shapes=[pltpu.VMEM((2, OBJ // 128 + 1, ROWS, 128), jnp.int32)],
        name="extract",
    )(offsets, half, other)


def substep(buf, order, rows, new, first, last):
    mids, laps = [], []
    for part in range(2):
        mid = [buf[order, part, j, pl.ds(rows - 1, R), :] for j in range(2)]
        far = [buf[order, part, j, pl.ds(rows - 2, R), :] for j in range(2)]
        left = [pltpu.roll(mid[j], 1, 1) for j in range(2)]
        right = [pltpu.roll(mid[j], 127, 1) for j in range(2)]
        left = [jnp.where(first, 0.0, left[0]), jnp.where(first, left[0], left[1])]
        right = [jnp.where(last, right[1], right[0]), jnp.where(last, 0.0, right[1])]
        mids.append(mid)
        laps.append([(far[j] + new[part][j]) + (left[j] + right[j]) - 4.0 * mid[j] for j in range(2)])
    new_re = [mids[0][j] + damping * laps[0][j] + turning * laps[1][j] for j in range(2)]
    new_im = [mids[1][j] + damping * laps[1][j] - turning * laps[0][j] for j in range(2)]
    return new_re, new_im


def sweep_kernel(
    windows, exit_ref, spr_ref, trans, inbox, spread_out, wave_out, waves, halves, tall, mine_only,
    own_sem, exit_sem, trans_sem, in_sem, spr_sem, trans_sent, spr_sent, wave_sent,
):
    sec = lax.axis_index("sec")
    scan = lax.axis_index("scan")
    group = sec // G
    member = lax.rem(sec, G)
    groups = lax.axis_size("sec") // G
    top = group == groups - 1

    def at(g, m):
        return (g * G + m, scan)

    barrier = pltpu.get_barrier_semaphore()
    for step in range(1, G):
        pl.semaphore_signal(barrier, 1, device_id=at(group, lax.rem(member + step, G)), device_id_type=MESH)

    @pl.when(group > 0)
    def _():
        pl.semaphore_signal(barrier, 1, device_id=at(group - 1, member), device_id_type=MESH)

    @pl.when(jnp.logical_not(top))
    def _():
        pl.semaphore_signal(barrier, 1, device_id=at(group + 1, member), device_id_type=MESH)

    pl.semaphore_wait(barrier, G - 1 + jnp.where(group > 0, 1, 0) + jnp.where(top, 0, 1))
    for order in range(G):
        waves[order, :, :, 0:8, :] = jnp.zeros((2, 2, 8, 128), jnp.float32)
        halves[order, :, :, 0:8, :] = jnp.zeros((2, 2, 8, 128), jnp.float32)
    inbox[:, W:, :] = jnp.zeros((2, S * R - W, W), jnp.bfloat16)
    mine = G - 1 - member

    def give(strip, unused):
        for step in range(1, G):
            person = lax.rem(member + step, G)
            pltpu.make_async_remote_copy(
                src_ref=windows.at[person, strip],
                dst_ref=trans.at[strip, mine],
                send_sem=trans_sent,
                recv_sem=trans_sem.at[strip],
                device_id=at(group, person),
                device_id_type=MESH,
            ).start()
        return unused

    lax.fori_loop(0, S, give, 0)

    ours = pltpu.make_async_copy(windows.at[member], mine_only, own_sem)
    ours.start()

    @pl.when(top)
    def _():
        exits = pltpu.make_async_copy(exit_ref.at[member], inbox.at[:, 0:W, :], exit_sem)
        exits.start()
        exits.wait()

    ours.wait()

    def own(strip, unused):
        trans[strip, mine] = mine_only[strip]
        return unused

    lax.fori_loop(0, S, own, 0)
    lane = lax.broadcasted_iota(jnp.int32, (R, 128), 1)
    first = lane == 0
    last = lane == 127
    row = lax.broadcasted_iota(jnp.int32, (R, 128), 0)

    def send_spread(strip, order):
        pltpu.make_async_remote_copy(
            src_ref=spread_out.at[strip, order],
            dst_ref=spr_ref.at[member, strip],
            send_sem=spr_sent,
            recv_sem=spr_sem,
            device_id=at(group, G - 1 - order),
            device_id_type=MESH,
        ).start()

    def one_strip(strip, unused):
        @pl.when(jnp.logical_and(strip < S - 1, jnp.logical_not(top)))
        def _():
            landed = inbox.at[:, pl.ds(pl.multiple_of(strip * R, R), R), :]
            pltpu.make_async_copy(landed, landed, in_sem.at[strip]).wait()

        pltpu.make_async_copy(
            trans.at[strip, 0 : G - 1], trans.at[strip, 0 : G - 1], trans_sem.at[strip]
        ).wait()
        before = jnp.maximum(strip - 1, 0)
        at_strip = pl.multiple_of(strip * R, R)
        rows = pl.multiple_of(8 + strip * R, 8)
        seen = pl.multiple_of(before * R, R)
        wave = [
            [inbox[part, pl.ds(at_strip, R), 128 * j : 128 * j + 128].astype(jnp.float32) for j in range(2)]
            for part in range(2)
        ]
        for order in range(G):
            for part in range(2):
                for j in range(2):
                    waves[order, part, j, pl.ds(rows, R), :] = wave[part][j]
            half = substep(waves, order, rows, wave, first, last)
            at_row = row + (strip * R - 2 * order - 1)
            inside = jnp.logical_and(at_row >= 0, at_row < W)
            half = [[jnp.where(inside, half[part][j], 0.0) for j in range(2)] for part in range(2)]
            for part in range(2):
                for j in range(2):
                    halves[order, part, j, pl.ds(rows, R), :] = half[part][j]
            spread_re, spread_im = substep(halves, order, rows, half, first, last)
            lag = 2 * (order + 1)
            wave = [[], []]
            for j in range(2):
                cols = slice(128 * j, 128 * j + 128)
                tall[order, 0, j, pl.ds(at_strip, R), :] = spread_re[j]
                tall[order, 1, j, pl.ds(at_strip, R), :] = spread_im[j]
                win_re = trans[strip, order, 0, :, cols].astype(jnp.int32).astype(jnp.float32)
                win_im = trans[strip, order, 1, :, cols].astype(jnp.int32).astype(jnp.float32)
                out_re = ((win_re * spread_re[j] + win_im * spread_im[j]) * (1.0 / FIX)).astype(jnp.bfloat16)
                out_im = ((win_re * spread_im[j] - win_im * spread_re[j]) * (1.0 / FIX)).astype(jnp.bfloat16)
                if order < G - 1:
                    wave[0].append(out_re.astype(jnp.float32))
                    wave[1].append(out_im.astype(jnp.float32))
                else:
                    wave_out[before, 0, :, cols] = out_re
                    wave_out[before, 1, :, cols] = out_im

        @pl.when(jnp.logical_and(strip > 0, group > 0))
        def _():
            pltpu.make_async_remote_copy(
                src_ref=wave_out.at[strip - 1],
                dst_ref=inbox.at[:, pl.ds(seen, R), :],
                send_sem=wave_sent,
                recv_sem=in_sem.at[strip - 1],
                device_id=at(group - 1, member),
                device_id_type=MESH,
            ).start()

        for order in range(G):
            lag = 2 * (order + 1)
            for part in range(2):
                for j in range(2):
                    spread_out[before, order, part, :, 128 * j : 128 * j + 128] = tall[
                        order, part, j, pl.ds(seen + lag, R), :
                    ].astype(jnp.bfloat16)

            @pl.when(jnp.logical_and(strip > 0, jnp.logical_and(group < LATE, member != G - 1 - order)))
            def _():
                send_spread(strip - 1, order)

        @pl.when(strip > 0)
        def _():
            spr_ref[member, strip - 1] = spread_out[strip - 1, mine]

        return unused

    lax.fori_loop(0, S, one_strip, 0)

    @pl.when(group >= LATE)
    def _():
        def rest(strip, unused):
            for order in range(G):

                @pl.when(member != G - 1 - order)
                def _():
                    send_spread(strip, order)

            return unused

        lax.fori_loop(0, S - 1, rest, 0)

    pltpu.make_async_copy(windows.at[0 : G - 1], windows.at[0 : G - 1], trans_sent).wait()
    pltpu.make_async_copy(spr_ref.at[0 : G - 1], spr_ref.at[0 : G - 1], spr_sent).wait()

    @pl.when(group > 0)
    def _():
        pltpu.make_async_copy(wave_out, wave_out, wave_sent).wait()

    pltpu.make_async_copy(spr_ref.at[0 : G - 1], spr_ref.at[0 : G - 1], spr_sem).wait()


def sweep(windows, exit_adjoint):
    return pl.pallas_call(
        sweep_kernel,
        out_shape=jax.ShapeDtypeStruct((G, S - 1, 2, R, W), jnp.bfloat16),
        in_specs=[pl.BlockSpec(memory_space=pl.ANY)] * 2,
        out_specs=pl.BlockSpec(memory_space=pltpu.VMEM),
        scratch_shapes=[
            pltpu.VMEM((S, G, 2, R, W), HELD),
            pltpu.VMEM((2, S * R, W), jnp.bfloat16),
            pltpu.VMEM((S - 1, G, 2, R, W), jnp.bfloat16),
            pltpu.VMEM((S - 1, 2, R, W), jnp.bfloat16),
            pltpu.VMEM((G, 2, 2, 8 + S * R, 128), jnp.float32),
            pltpu.VMEM((G, 2, 2, 8 + S * R, 128), jnp.float32),
            pltpu.VMEM((G, 2, 2, S * R, 128), jnp.float32),
            pltpu.VMEM((S, 2, R, W), HELD),
            pltpu.SemaphoreType.DMA,
            pltpu.SemaphoreType.DMA,
            pltpu.SemaphoreType.DMA((S,)),
            pltpu.SemaphoreType.DMA((S - 1,)),
            pltpu.SemaphoreType.DMA,
            pltpu.SemaphoreType.DMA,
            pltpu.SemaphoreType.DMA,
            pltpu.SemaphoreType.DMA,
        ],
        compiler_params=pltpu.CompilerParams(collective_id=0, has_side_effects=True),
        name="sweep",
    )(windows, exit_adjoint)


def gather_kernel(offs_ref, fwd_ref, spr_ref, leave_ref, keep_ref, acc):
    scan = lax.axis_index("scan")
    acc[...] = jnp.zeros_like(acc)
    lane = lax.broadcasted_iota(jnp.int32, (R, 128), 1)

    def per_position(position, unused):
        row_at = offs_ref[position, 0]
        col_at = offs_ref[position, 1]
        column = col_at // 128
        over = lax.rem(col_at, 128)
        keep = lane >= over

        def per_strip(strip, unused):
            rows = pl.ds(pl.multiple_of(strip * R, R), R)
            to = pl.ds(row_at + strip * R, R)
            terms = [[], []]
            for j in range(2):
                cols = slice(128 * j, 128 * j + 128)
                fwd_re = fwd_ref[position, 0, rows, cols].astype(jnp.float32)
                fwd_im = fwd_ref[position, 1, rows, cols].astype(jnp.float32)
                spread_re = spr_ref[position, strip, 0, :, cols].astype(jnp.float32)
                spread_im = spr_ref[position, strip, 1, :, cols].astype(jnp.float32)
                terms[0].append(pltpu.roll(fwd_re * spread_re + fwd_im * spread_im, over, 1))
                terms[1].append(pltpu.roll(fwd_re * spread_im - fwd_im * spread_re, over, 1))
            for part in range(2):
                near, far = terms[part]
                acc[part, column, to, :] += jnp.where(keep, near, 0.0)
                acc[part, column + 1, to, :] += jnp.where(keep, far, near)
                acc[part, column + 2, to, :] += jnp.where(keep, 0.0, far)
            return unused

        lax.fori_loop(0, S - 1, per_strip, 0, unroll=2)
        return unused

    lax.fori_loop(0, G, per_position, 0)

    def split(block, unused):
        rows = pl.ds(pl.multiple_of(block * BLOCK, BLOCK), BLOCK)
        ours = pl.ds(pl.multiple_of(scan * (OBJ // 2) + block * BLOCK, BLOCK), BLOCK)
        theirs = pl.ds(pl.multiple_of((1 - scan) * (OBJ // 2) + block * BLOCK, BLOCK), BLOCK)
        for part in range(2):
            for j in range(OBJ // 128):
                leave_ref[block, part, :, 128 * j : 128 * j + 128] = acc[part, j, theirs, :].astype(jnp.bfloat16)
                keep_ref[part, rows, 128 * j : 128 * j + 128] = acc[part, j, ours, :]
        return unused

    lax.fori_loop(0, BLOCKS, split, 0)


def gather(offsets, forward, spread):
    return pl.pallas_call(
        gather_kernel,
        out_shape=(
            jax.ShapeDtypeStruct((BLOCKS, 2, BLOCK, OBJ), jnp.bfloat16),
            jax.ShapeDtypeStruct((2, OBJ // 2, OBJ), jnp.float32),
        ),
        in_specs=[
            pl.BlockSpec(memory_space=pltpu.SMEM),
            pl.BlockSpec(memory_space=pltpu.VMEM),
            pl.BlockSpec(memory_space=pltpu.VMEM),
        ],
        out_specs=[pl.BlockSpec(memory_space=pltpu.VMEM)] * 2,
        scratch_shapes=[pltpu.VMEM((2, OBJ // 128 + 1, OBJ, 128), jnp.float32)],
        name="gather",
    )(offsets, forward, spread)


def reduce_kernel(leave_ref, keep_ref, out_ref, landing, sent, come):
    scan = lax.axis_index("scan")
    partner = (lax.axis_index("sec"), 1 - scan)
    barrier = pltpu.get_barrier_semaphore()
    pl.semaphore_signal(barrier, 1, device_id=partner, device_id_type=MESH)
    pl.semaphore_wait(barrier, 1)

    def chunk(block):
        return pltpu.make_async_remote_copy(
            src_ref=leave_ref.at[block],
            dst_ref=landing.at[block],
            send_sem=sent.at[block],
            recv_sem=come.at[block],
            device_id=partner,
            device_id_type=MESH,
        )

    def give(block, unused):
        chunk(block).start()
        return unused

    def join(block, unused):
        chunk(block).wait()
        rows = pl.ds(pl.multiple_of(block * BLOCK, BLOCK), BLOCK)
        out_ref[:, rows, :] = keep_ref[:, rows, :] + landing[block].astype(jnp.float32)
        return unused

    lax.fori_loop(0, BLOCKS, give, 0)
    lax.fori_loop(0, BLOCKS, join, 0)


def reduce(leave, keep):
    return pl.pallas_call(
        reduce_kernel,
        out_shape=jax.ShapeDtypeStruct((2, OBJ // 2, OBJ), jnp.float32),
        in_specs=[pl.BlockSpec(memory_space=pltpu.VMEM)] * 2,
        out_specs=pl.BlockSpec(memory_space=pltpu.VMEM),
        scratch_shapes=[
            pltpu.VMEM((BLOCKS, 2, BLOCK, OBJ), jnp.bfloat16),
            pltpu.SemaphoreType.DMA((BLOCKS,)),
            pltpu.SemaphoreType.DMA((BLOCKS,)),
        ],
        compiler_params=pltpu.CompilerParams(collective_id=2, has_side_effects=True),
        name="reduce",
    )(leave, keep)


def on_device(obj_amp, obj_phase, forward_waves, exit_adjoint, offsets):
    half, other = swap(obj_amp[0], obj_phase[0])
    spread = sweep(extract(offsets, half, other), exit_adjoint)
    leave, keep = gather(offsets, forward_waves[0], spread)
    return reduce(leave, keep)[None]


def solution(mesh):
    in_specs = (
        P("sec", "scan", None),
        P("sec", "scan", None),
        P("sec", "scan", None, None, None),
        P("scan", None, None, None),
        P("scan", None),
    )
    out_specs = P("sec", None, "scan", None)
    return jax.shard_map(
        on_device, mesh=mesh, in_specs=in_specs, out_specs=out_specs, check_vma=False
    )
```

time: 159 us -> 142 us (0.89)
  Pallas kernels: 150 us -> 139 us
  other arithmetic: 3.83 us -> 0 us
    pallas_call x1, Pallas kernels: 93.5 us -> 88.1 us  [sweep(): pl.pallas_call(sweep_kernel, out_shape=jax.ShapeDtypeStruct((G, S - 1, 2,...]
    pallas_call x2, Pallas kernels: 31.9 us -> 27.2 us  [the longest x1 17.7 us: swap(): pl.pallas_call(swap_kernel, out_shape=(rows, rows), in_specs=[pl.BlockSpe...]
    mul x1 -> x0, other arithmetic: 2.91 us -> none  [on_device(): obj_amp * jnp.cos(obj_phase)]
    unnamed x4 -> x2, local copies, waits for them, and re-layouts: 3.87 us -> 3.61 us
where the time goes in v3:
time: 142 us
  Pallas kernels  139 us (98%)
  local copies, waits for them, and re-layouts  3.61 us (3%)
    pallas_call x1, Pallas kernels, sweep(): pl.pallas_call(sweep_kernel, out_shape=jax.ShapeDtypeStruct((G, S - 1, 2,...  88.1 us
    pallas_call x1, Pallas kernels, swap(): pl.pallas_call(swap_kernel, out_shape=(rows, rows), in_specs=[pl.BlockSpe...  17.7 us
    pallas_call x1, Pallas kernels, reduce(): pl.pallas_call(reduce_kernel, out_shape=jax.ShapeDtypeStruct((2, OBJ // 2...  17.5 us
    pallas_call x1, Pallas kernels, gather(): pl.pallas_call(gather_kernel, out_shape=(jax.ShapeDtypeStruct((BLOCKS, 2,...  9.56 us
    pallas_call x1, Pallas kernels, extract(): pl.pallas_call(extract_kernel, out_shape=jax.ShapeDtypeStruct((G, S, 2, R...  5.81 us
    unnamed x2, local copies, waits for them, and re-layouts  3.61 us

profile of v3, /device:TPU:0, one launch (start us, length us, event | category | flops | bytes accessed | tf_op | source)
XLA Modules:
  0.0 142.2 jit_solution(11030161612527145316)
XLA Ops:
  0.0 1.3 copy.7.offs_ref
  1.3 17.7 %swap.1 = (s16[2,256,512]{2,1,0:T(8,128)(2,1)}, s16[2,256,512]{2,1,0:T(8,128)(2,1)}) custom-call(f32[256,512]{1,0:T(8,128)} %bitcast.6, f32[256,512]{1,0:T(8,128)} %bitcast.7), custom_call_target="tpu_custom_call" | custom-call | tf_op jit(solution)/shard_map/swap/pallas_call | solution.py:71
  19.0 5.8 %extract.1.windows = s16[8,17,2,16,256]{4,3,2,1,0:T(8,128)(2,1)} custom-call(s32[8,2]{1,0:T(8,128)} %copy.7.offs_ref, s16[2,256,512]{2,1,0:T(8,128)(2,1)} %get-tuple-element.9.half_ref, s16[2,256,512]{2,1,0:T(8,128)(2,1)} %get-tuple-element.10.other_ref), custom_call_target="tpu_custom_call" | custom-call | tf_op jit(solution)/shard_map/extract/pallas_call | solution.py:123
  24.8 88.1 %sweep.1.spr_ref = bf16[8,16,2,16,256]{4,3,2,1,0:T(8,128)(2,1)} custom-call(s16[8,17,2,16,256]{4,3,2,1,0:T(8,128)(2,1)} %extract.1.windows, bf16[8,2,256,256]{3,2,1,0:T(8,128)(2,1)} %exit_ref.1), custom_call_target="tpu_custom_call" | custom-call | tf_op jit(solution)/shard_map/sweep/pallas_call | solution.py:333
  112.9 9.6 %gather.1 = (bf16[8,2,32,512]{3,2,1,0:T(8,128)(2,1)}, f32[2,256,512]{2,1,0:T(8,128)}) custom-call(s32[8,2]{1,0:T(8,128)} %copy.7.offs_ref, bf16[8,2,256,256]{3,2,1,0:T(8,128)(2,1)} %bitcast.5, bf16[8,16,2,16,256]{4,3,2,1,0:T(8,128)(2,1)} %sweep.1.spr_ref), custom_call_target="tpu_custom_call" | custom-call | tf_op jit(solution)/shard_map/gather/pallas_call | solution.py:411
  122.4 17.5 %reduce.1 = f32[2,256,512]{2,1,0:T(8,128)} custom-call(bf16[8,2,32,512]{3,2,1,0:T(8,128)(2,1)} %get-tuple-element.11.leave_ref, f32[2,256,512]{2,1,0:T(8,128)} %get-tuple-element.12.keep_ref), custom_call_target="tpu_custom_call" | custom-call | tf_op jit(solution)/shard_map/reduce/pallas_call | solution.py:460
  139.9 2.3 %copy.9 = f32[1,2,256,512]{3,2,1,0:T(8,128)} copy(f32[1,2,256,512]{3,2,1,0:T(8,128)} %bitcast.4) | data formatting | bytes 2097152

commit v4 on v3

--- a/solution.py
+++ b/solution.py
@@ -24,6 +24,7 @@
 COLS = OBJ + 128
 FIX = 32767.0
 HELD = jnp.int16
+RUN = 64
 BLOCK = 32
 BLOCKS = OBJ // 2 // BLOCK
 
@@ -134,24 +135,61 @@
     )(offsets, half, other)
 
 
-def substep(buf, order, rows, new, first, last):
-    mids, laps = [], []
+def behind(carry, at, value):
+    top = lax.broadcasted_iota(jnp.int32, (8, 128), 0) < 1
+    pieces = [carry[at]] + [value[8 * i : 8 * i + 8] for i in range(R // 8)]
+    carry[at] = pieces[-1]
+    rolled = [pltpu.roll(piece, 1, 0) for piece in pieces]
+    return jnp.concatenate([jnp.where(top, rolled[i], rolled[i + 1]) for i in range(R // 8)], axis=0)
+
+
+def times(re, im, value, j):
+    return re * value[0][j] + im * value[1][j], re * value[1][j] - im * value[0][j]
+
+
+def both_steps(carry, order, wave, inside, lane):
+    sums, squares, here = [[], []], [[], []], [[], []]
     for part in range(2):
-        mid = [buf[order, part, j, pl.ds(rows - 1, R), :] for j in range(2)]
-        far = [buf[order, part, j, pl.ds(rows - 2, R), :] for j in range(2)]
-        left = [pltpu.roll(mid[j], 1, 1) for j in range(2)]
-        right = [pltpu.roll(mid[j], 127, 1) for j in range(2)]
-        left = [jnp.where(first, 0.0, left[0]), jnp.where(first, left[0], left[1])]
-        right = [jnp.where(last, right[1], right[0]), jnp.where(last, 0.0, right[1])]
-        mids.append(mid)
-        laps.append([(far[j] + new[part][j]) + (left[j] + right[j]) - 4.0 * mid[j] for j in range(2)])
-    new_re = [mids[0][j] + damping * laps[0][j] + turning * laps[1][j] for j in range(2)]
-    new_im = [mids[1][j] + damping * laps[1][j] - turning * laps[0][j] for j in range(2)]
-    return new_re, new_im
+        v = wave[part]
+        left1, left2 = ([pltpu.roll(v[j], n, 1) for j in range(2)] for n in (1, 2))
+        right1, right2 = ([pltpu.roll(v[j], 128 - n, 1) for j in range(2)] for n in (1, 2))
+
+        def pair(left, right, n):
+            low, high = lane < n, lane >= 128 - n
+            return [
+                jnp.where(low, 0.0, left[0]) + jnp.where(high, right[1], right[0]),
+                jnp.where(low, left[0], left[1]) + jnp.where(high, 0.0, right[1]),
+            ]
+
+        h = pair(left1, right1, 1)
+        g = pair(left2, right2, 2)
+        own = [jnp.where(lane == 0, 1.0, 2.0), jnp.where(lane == 127, 1.0, 2.0)]
+        for j in range(2):
+            g[j] = g[j] + own[j] * v[j]
+            two = behind(carry, (order, 0, part, j), v[j])
+            one = behind(carry, (order, 1, part, j), (h[j] - 4.0 * v[j]) + two)
+            here[part].append(jnp.where(inside, v[j] + one, 0.0))
+        sums[part] = h
+        squares[part] = g
+    square_re, square_im = damping * damping - turning * turning, 2.0 * damping * turning
+    first_re, first_im = 2.0 * damping - 4.0 * square_re, 2.0 * turning - 4.0 * square_im
+    inner = [[here[part][j] + squares[part][j] - 4.0 * sums[part][j] for j in range(2)] for part in range(2)]
+    spread = [[], []]
+    for j in range(2):
+        last = times(square_re, square_im, here, j)
+        middle = times(first_re, first_im, here, j)
+        edge = times(square_re, square_im, sums, j)
+        core = times(square_re, square_im, inner, j)
+        for part in range(2):
+            third = behind(carry, (order, 2, part, j), edge[part])
+            second = behind(carry, (order, 3, part, j), (wave[part][j] + core[part]) + third)
+            whole = behind(carry, (order, 4, part, j), (middle[part] + edge[part]) + second)
+            spread[part].append(last[part] + whole)
+    return spread
 
 
 def sweep_kernel(
-    windows, exit_ref, spr_ref, trans, inbox, spread_out, wave_out, waves, halves, tall, mine_only,
+    windows, exit_ref, spr_ref, trans, inbox, spread_out, wave_out, waves, tall, mine_only,
     own_sem, exit_sem, trans_sem, in_sem, spr_sem, trans_sent, spr_sent, wave_sent,
 ):
     sec = lax.axis_index("sec")
@@ -177,9 +215,7 @@
         pl.semaphore_signal(barrier, 1, device_id=at(group + 1, member), device_id_type=MESH)
 
     pl.semaphore_wait(barrier, G - 1 + jnp.where(group > 0, 1, 0) + jnp.where(top, 0, 1))
-    for order in range(G):
-        waves[order, :, :, 0:8, :] = jnp.zeros((2, 2, 8, 128), jnp.float32)
-        halves[order, :, :, 0:8, :] = jnp.zeros((2, 2, 8, 128), jnp.float32)
+    waves[...] = jnp.zeros_like(waves)
     inbox[:, W:, :] = jnp.zeros((2, S * R - W, W), jnp.bfloat16)
     mine = G - 1 - member
 
@@ -215,8 +251,6 @@
 
     lax.fori_loop(0, S, own, 0)
     lane = lax.broadcasted_iota(jnp.int32, (R, 128), 1)
-    first = lane == 0
-    last = lane == 127
     row = lax.broadcasted_iota(jnp.int32, (R, 128), 0)
 
     def send_spread(strip, order):
@@ -240,25 +274,15 @@
         ).wait()
         before = jnp.maximum(strip - 1, 0)
         at_strip = pl.multiple_of(strip * R, R)
-        rows = pl.multiple_of(8 + strip * R, 8)
         seen = pl.multiple_of(before * R, R)
         wave = [
             [inbox[part, pl.ds(at_strip, R), 128 * j : 128 * j + 128].astype(jnp.float32) for j in range(2)]
             for part in range(2)
         ]
         for order in range(G):
-            for part in range(2):
-                for j in range(2):
-                    waves[order, part, j, pl.ds(rows, R), :] = wave[part][j]
-            half = substep(waves, order, rows, wave, first, last)
             at_row = row + (strip * R - 2 * order - 1)
             inside = jnp.logical_and(at_row >= 0, at_row < W)
-            half = [[jnp.where(inside, half[part][j], 0.0) for j in range(2)] for part in range(2)]
-            for part in range(2):
-                for j in range(2):
-                    halves[order, part, j, pl.ds(rows, R), :] = half[part][j]
-            spread_re, spread_im = substep(halves, order, rows, half, first, last)
-            lag = 2 * (order + 1)
+            spread_re, spread_im = both_steps(waves, order, wave, inside, lane)
             wave = [[], []]
             for j in range(2):
                 cols = slice(128 * j, 128 * j + 128)
@@ -340,8 +364,7 @@
             pltpu.VMEM((2, S * R, W), jnp.bfloat16),
             pltpu.VMEM((S - 1, G, 2, R, W), jnp.bfloat16),
             pltpu.VMEM((S - 1, 2, R, W), jnp.bfloat16),
-            pltpu.VMEM((G, 2, 2, 8 + S * R, 128), jnp.float32),
-            pltpu.VMEM((G, 2, 2, 8 + S * R, 128), jnp.float32),
+            pltpu.VMEM((G, 5, 2, 2, 8, 128), jnp.float32),
             pltpu.VMEM((G, 2, 2, S * R, 128), jnp.float32),
             pltpu.VMEM((S, 2, R, W), HELD),
             pltpu.SemaphoreType.DMA,
@@ -358,10 +381,11 @@
     )(windows, exit_adjoint)
 
 
-def gather_kernel(offs_ref, fwd_ref, spr_ref, leave_ref, keep_ref, acc):
+def gather_kernel(other, offs_ref, fwd_ref, spr_ref, grad_ref, acc):
     scan = lax.axis_index("scan")
+    start = ((1 - scan) if other else scan) * (OBJ // 2)
     acc[...] = jnp.zeros_like(acc)
-    lane = lax.broadcasted_iota(jnp.int32, (R, 128), 1)
+    lane = lax.broadcasted_iota(jnp.int32, (RUN, 128), 1)
 
     def per_position(position, unused):
         row_at = offs_ref[position, 0]
@@ -369,17 +393,22 @@
         column = col_at // 128
         over = lax.rem(col_at, 128)
         keep = lane >= over
-
-        def per_strip(strip, unused):
-            rows = pl.ds(pl.multiple_of(strip * R, R), R)
-            to = pl.ds(row_at + strip * R, R)
+        begin = jnp.maximum(start - row_at, 0) // RUN
+        end = jnp.minimum((start + OBJ // 2 - row_at + RUN - 1) // RUN, W // RUN)
+
+        def per_run(run, unused):
+            rows = pl.ds(pl.multiple_of(run * RUN, RUN), RUN)
+            to = pl.ds(row_at + run * RUN - start + RUN, RUN)
             terms = [[], []]
             for j in range(2):
                 cols = slice(128 * j, 128 * j + 128)
                 fwd_re = fwd_ref[position, 0, rows, cols].astype(jnp.float32)
                 fwd_im = fwd_ref[position, 1, rows, cols].astype(jnp.float32)
-                spread_re = spr_ref[position, strip, 0, :, cols].astype(jnp.float32)
-                spread_im = spr_ref[position, strip, 1, :, cols].astype(jnp.float32)
+                spread = [
+                    jnp.concatenate([spr_ref[position, run * (RUN // R) + i, part, :, cols] for i in range(RUN // R)], axis=0)
+                    for part in range(2)
+                ]
+                spread_re, spread_im = (part.astype(jnp.float32) for part in spread)
                 terms[0].append(pltpu.roll(fwd_re * spread_re + fwd_im * spread_im, over, 1))
                 terms[1].append(pltpu.roll(fwd_re * spread_im - fwd_im * spread_re, over, 1))
             for part in range(2):
@@ -389,94 +418,45 @@
                 acc[part, column + 2, to, :] += jnp.where(keep, 0.0, far)
             return unused
 
-        lax.fori_loop(0, S - 1, per_strip, 0, unroll=2)
+        lax.fori_loop(begin, end, per_run, 0)
         return unused
 
     lax.fori_loop(0, G, per_position, 0)
 
     def split(block, unused):
         rows = pl.ds(pl.multiple_of(block * BLOCK, BLOCK), BLOCK)
-        ours = pl.ds(pl.multiple_of(scan * (OBJ // 2) + block * BLOCK, BLOCK), BLOCK)
-        theirs = pl.ds(pl.multiple_of((1 - scan) * (OBJ // 2) + block * BLOCK, BLOCK), BLOCK)
+        source = pl.ds(pl.multiple_of(RUN + block * BLOCK, BLOCK), BLOCK)
         for part in range(2):
             for j in range(OBJ // 128):
-                leave_ref[block, part, :, 128 * j : 128 * j + 128] = acc[part, j, theirs, :].astype(jnp.bfloat16)
-                keep_ref[part, rows, 128 * j : 128 * j + 128] = acc[part, j, ours, :]
+                grad_ref[part, rows, 128 * j : 128 * j + 128] = acc[part, j, source, :].astype(grad_ref.dtype)
         return unused
 
     lax.fori_loop(0, BLOCKS, split, 0)
 
 
-def gather(offsets, forward, spread):
+def gather(offsets, forward, spread, other):
     return pl.pallas_call(
-        gather_kernel,
-        out_shape=(
-            jax.ShapeDtypeStruct((BLOCKS, 2, BLOCK, OBJ), jnp.bfloat16),
-            jax.ShapeDtypeStruct((2, OBJ // 2, OBJ), jnp.float32),
-        ),
+        functools.partial(gather_kernel, other),
+        out_shape=jax.ShapeDtypeStruct((2, OBJ // 2, OBJ), jnp.bfloat16 if other else jnp.float32),
         in_specs=[
             pl.BlockSpec(memory_space=pltpu.SMEM),
             pl.BlockSpec(memory_space=pltpu.VMEM),
             pl.BlockSpec(memory_space=pltpu.VMEM),
         ],
-        out_specs=[pl.BlockSpec(memory_space=pltpu.VMEM)] * 2,
-        scratch_shapes=[pltpu.VMEM((2, OBJ // 128 + 1, OBJ, 128), jnp.float32)],
-        name="gather",
+        out_specs=pl.BlockSpec(memory_space=pltpu.VMEM),
+        scratch_shapes=[pltpu.VMEM((2, OBJ // 128 + 1, OBJ // 2 + 2 * RUN, 128), jnp.float32)],
+        cost_estimate=pl.CostEstimate(flops=20_000_000, bytes_accessed=6_000_000, transcendentals=0),
+        name="gather_other" if other else "gather_own",
     )(offsets, forward, spread)
-
-
-def reduce_kernel(leave_ref, keep_ref, out_ref, landing, sent, come):
-    scan = lax.axis_index("scan")
-    partner = (lax.axis_index("sec"), 1 - scan)
-    barrier = pltpu.get_barrier_semaphore()
-    pl.semaphore_signal(barrier, 1, device_id=partner, device_id_type=MESH)
-    pl.semaphore_wait(barrier, 1)
-
-    def chunk(block):
-        return pltpu.make_async_remote_copy(
-            src_ref=leave_ref.at[block],
-            dst_ref=landing.at[block],
-            send_sem=sent.at[block],
-            recv_sem=come.at[block],
-            device_id=partner,
-            device_id_type=MESH,
-        )
-
-    def give(block, unused):
-        chunk(block).start()
-        return unused
-
-    def join(block, unused):
-        chunk(block).wait()
-        rows = pl.ds(pl.multiple_of(block * BLOCK, BLOCK), BLOCK)
-        out_ref[:, rows, :] = keep_ref[:, rows, :] + landing[block].astype(jnp.float32)
-        return unused
-
-    lax.fori_loop(0, BLOCKS, give, 0)
-    lax.fori_loop(0, BLOCKS, join, 0)
-
-
-def reduce(leave, keep):
-    return pl.pallas_call(
-        reduce_kernel,
-        out_shape=jax.ShapeDtypeStruct((2, OBJ // 2, OBJ), jnp.float32),
-        in_specs=[pl.BlockSpec(memory_space=pltpu.VMEM)] * 2,
-        out_specs=pl.BlockSpec(memory_space=pltpu.VMEM),
-        scratch_shapes=[
-            pltpu.VMEM((BLOCKS, 2, BLOCK, OBJ), jnp.bfloat16),
-            pltpu.SemaphoreType.DMA((BLOCKS,)),
-            pltpu.SemaphoreType.DMA((BLOCKS,)),
-        ],
-        compiler_params=pltpu.CompilerParams(collective_id=2, has_side_effects=True),
-        name="reduce",
-    )(leave, keep)
 
 
 def on_device(obj_amp, obj_phase, forward_waves, exit_adjoint, offsets):
     half, other = swap(obj_amp[0], obj_phase[0])
     spread = sweep(extract(offsets, half, other), exit_adjoint)
-    leave, keep = gather(offsets, forward_waves[0], spread)
-    return reduce(leave, keep)[None]
+    leave = gather(offsets, forward_waves[0], spread, True)
+    come = lax.ppermute(leave, "scan", [(0, 1), (1, 0)])
+    keep = gather(offsets, forward_waves[0], spread, False)
+    return (keep + come.astype(jnp.float32))[None]
 
 
 def solution(mesh):

time: 142 us -> 124 us (0.87)
  Pallas kernels: 139 us -> 111 us
  waiting for transfers between devices: 0 us -> 7.52 us
  other arithmetic: 0 us -> 2.37 us
  local copies, waits for them, and re-layouts: 3.61 us -> 1.34 us
  starting transfers between devices: 0 us -> 2.11 us
    pallas_call x2, Pallas kernels: 27.1 us -> 11.3 us  [gather(): pl.pallas_call(functools.partial(gather_kernel, other), out_shape=jax.Sha...]
    pallas_call x1, Pallas kernels: 88.1 us -> 75.8 us  [sweep(): pl.pallas_call(sweep_kernel, out_shape=jax.ShapeDtypeStruct((G, S - 1, 2,...]
    ppermute x0 -> x1, waiting for transfers between devices: none -> 7.52 us  [on_device(): come = lax.ppermute(leave, 'scan', [(0, 1), (1, 0)])]
    broadcast_in_dim x0 -> x1, other arithmetic: none -> 2.37 us  [on_device(): return (keep + come.astype(jnp.float32))[None]]
    unnamed x2 -> x1, local copies, waits for them, and re-layouts: 3.61 us -> 1.34 us
    ppermute x0 -> x1, starting transfers between devices: none -> 2.11 us  [on_device(): come = lax.ppermute(leave, 'scan', [(0, 1), (1, 0)])]
  transfers between devices with their start and end apart: 0 -> 1, of which waited for: 0 -> 1; matrix products, arithmetic and copies ran while one was open for 0% -> 0% of each run, Pallas kernels for 0% -> 4%
where the time goes in v4:
time: 124 us
  Pallas kernels  111 us (90%)
  waiting for transfers between devices  7.52 us (6%)
  other arithmetic  2.37 us (2%)
  starting transfers between devices  2.11 us (2%)
  local copies, waits for them, and re-layouts  1.34 us (1%)
    pallas_call x1, Pallas kernels, sweep(): pl.pallas_call(sweep_kernel, out_shape=jax.ShapeDtypeStruct((G, S - 1, 2,...  75.8 us
    pallas_call x1, Pallas kernels, swap(): pl.pallas_call(swap_kernel, out_shape=(rows, rows), in_specs=[pl.BlockSpe...  17.7 us
    pallas_call x2, Pallas kernels, gather(): pl.pallas_call(functools.partial(gather_kernel, other), out_shape=jax.Sha...  11.3 us
    ppermute x1, waiting for transfers between devices, on_device(): come = lax.ppermute(leave, 'scan', [(0, 1), (1, 0)])  7.52 us
    pallas_call x1, Pallas kernels, extract(): pl.pallas_call(extract_kernel, out_shape=jax.ShapeDtypeStruct((G, S, 2, R...  5.8 us
  transfers between devices with their start and end apart: 1, of which 1 were waited for; matrix products, arithmetic and copies ran while one was open for 0% of the time, Pallas kernels for 4%

profile of v4, /device:TPU:0, one launch (start us, length us, event | category | flops | bytes accessed | tf_op | source)
XLA Modules:
  0.0 123.9 jit_solution(3166539229276423452)
XLA Ops:
  0.0 1.3 %copy.7.offs_ref = s32[8,2]{1,0:T(8,128)} copy(s32[8,2]{0,1:T(2,128)} %param.9) | data formatting | bytes 128 | tf_op args[4]
  1.3 17.7 %swap.1 = (s16[2,256,512]{2,1,0:T(8,128)(2,1)}, s16[2,256,512]{2,1,0:T(8,128)(2,1)}) custom-call(f32[256,512]{1,0:T(8,128)} %bitcast.7, f32[256,512]{1,0:T(8,128)} %bitcast.8), custom_call_target="tpu_custom_call" | custom-call | tf_op jit(solution)/shard_map/swap/pallas_call | solution.py:72
  19.0 5.8 %extract.1.windows = s16[8,17,2,16,256]{4,3,2,1,0:T(8,128)(2,1)} custom-call(s32[8,2]{1,0:T(8,128)} %copy.7.offs_ref, s16[2,256,512]{2,1,0:T(8,128)(2,1)} %get-tuple-element.7.half_ref, s16[2,256,512]{2,1,0:T(8,128)(2,1)} %get-tuple-element.8.other_ref), custom_call_target="tpu_custom_call" | custom-call | tf_op jit(solution)/shard_map/extract/pallas_call | solution.py:124
  24.8 75.8 %sweep.1.spr_ref = bf16[8,16,2,16,256]{4,3,2,1,0:T(8,128)(2,1)} custom-call(s16[8,17,2,16,256]{4,3,2,1,0:T(8,128)(2,1)} %extract.1.windows, bf16[8,2,256,256]{3,2,1,0:T(8,128)(2,1)} %exit_ref.1), custom_call_target="tpu_custom_call" | custom-call | tf_op jit(solution)/shard_map/sweep/pallas_call | solution.py:357
  100.6 5.8 %gather_other.1 = bf16[2,256,512]{2,1,0:T(8,128)(2,1)} custom-call(s32[8,2]{1,0:T(8,128)} %copy.7.offs_ref, bf16[8,2,256,256]{3,2,1,0:T(8,128)(2,1)} %bitcast.5, bf16[8,16,2,16,256]{4,3,2,1,0:T(8,128)(2,1)} %sweep.1.spr_ref), custom_call_target="tpu_custom_call" | custom-call | flops 20000000 | bytes 6000000 | tf_op jit(solution)/shard_map/gather_other/pallas_call | solution.py:438
  106.4 2.1 %collective-permute-start = (bf16[2,256,512]{2,1,0:T(8,128)(2,1)}, bf16[2,256,512]{2,1,0:T(8,128)(2,1)S(1)}, u32[]{:S(2)}, u32[]{:S(2)}) collective-permute-start(bf16[2,256,512]{2,1,0:T(8,128)(2,1)} %gather_other.1), channel_id=1, source_target_pairs={{0,1},{1,0},{2,3},{3,2},{4,5},{5,4},{6,7},{7,6},{8,9},{9,8},{10,11... | collective-permute-start | bytes 1572872 | tf_op jit(solution)/shard_map/ppermute | solution.py:457
  108.5 5.5 %gather_own.1 = f32[2,256,512]{2,1,0:T(8,128)} custom-call(s32[8,2]{1,0:T(8,128)} %copy.7.offs_ref, bf16[8,2,256,256]{3,2,1,0:T(8,128)(2,1)} %bitcast.6, bf16[8,16,2,16,256]{4,3,2,1,0:T(8,128)(2,1)} %sweep.1.spr_ref), custom_call_target="tpu_custom_call" | custom-call | flops 20000000 | bytes 6000000 | tf_op jit(solution)/shard_map/gather_own/pallas_call | solution.py:438
  114.0 7.5 %collective-permute-done = bf16[2,256,512]{2,1,0:T(8,128)(2,1)S(1)} collective-permute-done((bf16[2,256,512]{2,1,0:T(8,128)(2,1)}, bf16[2,256,512]{2,1,0:T(8,128)(2,1)S(1)}, u32[]{:S(2)}, u32[]{:S(2)}) %collective-permute-start) | collective-permute-done | bytes 524320 | tf_op jit(solution)/shard_map/ppermute | solution.py:457
  121.5 2.4 %add_bitcast_fusion = f32[1,2,256,512]{3,2,1,0:T(8,128)} fusion(f32[2,256,512]{2,1,0:T(8,128)} %gather_own.1, bf16[2,256,512]{2,1,0:T(8,128)(2,1)S(1)} %collective-permute-done), kind=kLoop, calls=%fused_computation | loop fusion | flops 524288 | bytes 2621440 | tf_op jit(solution)/shard_map/broadcast_in_dim | solution.py:459
Async XLA Ops:
  106.4 15.2 %collective-permute-start = (bf16[2,256,512]{2,1,0:T(8,128)(2,1)}, bf16[2,256,512]{2,1,0:T(8,128)(2,1)S(1)}, u32[]{:S(2)}, u32[]{:S(2)}) collective-permute-start(bf16[2,256,512]{2,1,0:T(8,128)(2,1)} %gather_other.1), channel_id=1, source_target_pairs={{0,1},{1,0},{2,3},{3,2},{4,5},{5,4},{6,7},{7,6},{8,9},{9,8},{10,11... | collective-permute-start | bytes 1572872 | tf_op jit(solution)/shard_map/ppermute | solution.py:457

commit v5 on v4

--- a/solution.py
+++ b/solution.py
@@ -27,112 +27,6 @@
 RUN = 64
 BLOCK = 32
 BLOCKS = OBJ // 2 // BLOCK
-
-
-def swap_kernel(amp_ref, phase_ref, half_ref, other_ref, sent, come):
-    partner = (lax.axis_index("sec"), 1 - lax.axis_index("scan"))
-    barrier = pltpu.get_barrier_semaphore()
-    pl.semaphore_signal(barrier, 1, device_id=partner, device_id_type=MESH)
-    pl.semaphore_wait(barrier, 1)
-
-    def chunk(block):
-        rows = pl.ds(pl.multiple_of(block * BLOCK, BLOCK), BLOCK)
-        return pltpu.make_async_remote_copy(
-            src_ref=half_ref.at[:, rows, :],
-            dst_ref=other_ref.at[:, rows, :],
-            send_sem=sent.at[block],
-            recv_sem=come.at[block],
-            device_id=partner,
-            device_id_type=MESH,
-        )
-
-    def fixed(value):
-        value = value * FIX
-        return jnp.where(value >= 0.0, value + 0.5, value - 0.5).astype(jnp.int32).astype(HELD)
-
-    def give(block, unused):
-        rows = pl.ds(pl.multiple_of(block * BLOCK, BLOCK), BLOCK)
-        amp = amp_ref[rows, :]
-        phase = phase_ref[rows, :]
-        half_ref[0, rows, :] = fixed(amp * jnp.cos(phase))
-        half_ref[1, rows, :] = fixed(amp * jnp.sin(phase))
-        chunk(block).start()
-        return unused
-
-    def take(block, unused):
-        chunk(block).wait()
-        return unused
-
-    lax.fori_loop(0, BLOCKS, give, 0)
-    lax.fori_loop(0, BLOCKS, take, 0)
-
-
-def swap(amp, phase):
-    rows = jax.ShapeDtypeStruct((2, OBJ // 2, OBJ), HELD)
-    return pl.pallas_call(
-        swap_kernel,
-        out_shape=(rows, rows),
-        in_specs=[pl.BlockSpec(memory_space=pltpu.VMEM)] * 2,
-        out_specs=[pl.BlockSpec(memory_space=pltpu.VMEM)] * 2,
-        scratch_shapes=[pltpu.SemaphoreType.DMA((BLOCKS,)), pltpu.SemaphoreType.DMA((BLOCKS,))],
-        compiler_params=pltpu.CompilerParams(collective_id=1, has_side_effects=True),
-        name="swap",
-    )(amp, phase)
-
-
-def extract_kernel(offs_ref, half_ref, other_ref, win_ref, padded):
-    scan = lax.axis_index("scan")
-    order = G - 1 - lax.rem(lax.axis_index("sec"), G)
-    delay = 2 * (order + 1)
-
-    def place(source, start):
-        def some_rows(block, unused):
-            rows = pl.ds(pl.multiple_of(block * BLOCK, BLOCK), BLOCK)
-            to = pl.ds(pl.multiple_of(start + block * BLOCK, 8), BLOCK)
-            for part in range(2):
-                for j in range(OBJ // 128):
-                    padded[part, j, to, :] = source[part, rows, 128 * j : 128 * j + 128].astype(jnp.int32)
-            return unused
-
-        lax.fori_loop(0, BLOCKS, some_rows, 0)
-
-    place(half_ref, pl.multiple_of(TOP + scan * (OBJ // 2), 8))
-    place(other_ref, pl.multiple_of(TOP + (1 - scan) * (OBJ // 2), 8))
-    lane = lax.broadcasted_iota(jnp.int32, (R, 128), 1)
-
-    def per_strip(strip, unused):
-        at = lax.broadcasted_iota(jnp.int32, (R, 128), 0) + (strip * R - delay)
-        inside = jnp.logical_and(at >= 0, at < W)
-        for position in range(G):
-            col_at = offs_ref[position, 1]
-            column = col_at // 128
-            over = lax.rem(col_at, 128)
-            turn = lax.rem(128 - over, 128)
-            keep = lane < 128 - over
-            rows = pl.ds(offs_ref[position, 0] + (strip * R - delay + TOP), R)
-            for part in range(2):
-                rolled = [pltpu.roll(padded[part, column + j, rows, :], turn, 1) for j in range(3)]
-                for j in range(2):
-                    value = jnp.where(inside, jnp.where(keep, rolled[j], rolled[j + 1]), 0)
-                    win_ref[position, strip, part, :, 128 * j : 128 * j + 128] = value.astype(HELD)
-        return unused
-
-    lax.fori_loop(0, S, per_strip, 0)
-
-
-def extract(offsets, half, other):
-    return pl.pallas_call(
-        extract_kernel,
-        out_shape=jax.ShapeDtypeStruct((G, S, 2, R, W), HELD),
-        in_specs=[
-            pl.BlockSpec(memory_space=pltpu.SMEM),
-            pl.BlockSpec(memory_space=pltpu.VMEM),
-            pl.BlockSpec(memory_space=pltpu.VMEM),
-        ],
-        out_specs=pl.BlockSpec(memory_space=pltpu.VMEM),
-        scratch_shapes=[pltpu.VMEM((2, OBJ // 128 + 1, ROWS, 128), jnp.int32)],
-        name="extract",
-    )(offsets, half, other)
 
 
 def behind(carry, at, value):
@@ -189,8 +83,8 @@
 
 
 def sweep_kernel(
-    windows, exit_ref, spr_ref, trans, inbox, spread_out, wave_out, waves, tall, mine_only,
-    own_sem, exit_sem, trans_sem, in_sem, spr_sem, trans_sent, spr_sent, wave_sent,
+    plan_ref, amp_ref, phase_ref, exit_ref, spr_ref, half, other, padded, windows, trans, inbox, spread_out, wave_out, waves, tall,
+    half_sem, half_sent, exit_sem, trans_sem, in_sem, spr_sem, trans_sent, spr_sent, wave_sent,
 ):
     sec = lax.axis_index("sec")
     scan = lax.axis_index("scan")
@@ -206,6 +100,9 @@
     for step in range(1, G):
         pl.semaphore_signal(barrier, 1, device_id=at(group, lax.rem(member + step, G)), device_id_type=MESH)
 
+    partner = (sec, 1 - scan)
+    pl.semaphore_signal(barrier, 1, device_id=partner, device_id_type=MESH)
+
     @pl.when(group > 0)
     def _():
         pl.semaphore_signal(barrier, 1, device_id=at(group - 1, member), device_id_type=MESH)
@@ -214,43 +111,88 @@
     def _():
         pl.semaphore_signal(barrier, 1, device_id=at(group + 1, member), device_id_type=MESH)
 
-    pl.semaphore_wait(barrier, G - 1 + jnp.where(group > 0, 1, 0) + jnp.where(top, 0, 1))
+    pl.semaphore_wait(barrier, G + jnp.where(group > 0, 1, 0) + jnp.where(top, 0, 1))
+    mine = G - 1 - member
+    delay = 2 * (mine + 1)
+    exits = pltpu.make_async_copy(exit_ref.at[member], inbox.at[:, 0:W, :], exit_sem)
+
+    @pl.when(top)
+    def _():
+        exits.start()
+
+    def block_rows(block):
+        return pl.ds(pl.multiple_of(block * BLOCK, BLOCK), BLOCK)
+
+    def chunk(part, block):
+        return pltpu.make_async_remote_copy(
+            src_ref=half.at[part, block_rows(block), :],
+            dst_ref=other.at[part, block_rows(block), :],
+            send_sem=half_sent.at[part, block],
+            recv_sem=half_sem.at[part, block],
+            device_id=partner,
+            device_id_type=MESH,
+        )
+
+    def place(part, block, value, owner):
+        to = pl.ds(pl.multiple_of(TOP + owner * (OBJ // 2) + block * BLOCK, 8), BLOCK)
+        for j in range(OBJ // 128):
+            padded[part, j, to, :] = value[:, 128 * j : 128 * j + 128]
+
+    for part, wave in enumerate((jnp.cos, jnp.sin)):
+
+        def make(block, unused):
+            value = amp_ref[block_rows(block), :] * wave(phase_ref[block_rows(block), :]) * FIX
+            value = jnp.where(value >= 0.0, value + 0.5, value - 0.5).astype(jnp.int32)
+            half[part, block_rows(block), :] = value.astype(HELD)
+            chunk(part, block).start()
+            place(part, block, value, scan)
+            return unused
+
+        lax.fori_loop(0, BLOCKS, make, 0)
     waves[...] = jnp.zeros_like(waves)
     inbox[:, W:, :] = jnp.zeros((2, S * R - W, W), jnp.bfloat16)
-    mine = G - 1 - member
-
-    def give(strip, unused):
-        for step in range(1, G):
-            person = lax.rem(member + step, G)
-            pltpu.make_async_remote_copy(
-                src_ref=windows.at[person, strip],
-                dst_ref=trans.at[strip, mine],
-                send_sem=trans_sent,
-                recv_sem=trans_sem.at[strip],
-                device_id=at(group, person),
-                device_id_type=MESH,
-            ).start()
-        return unused
-
-    lax.fori_loop(0, S, give, 0)
-
-    ours = pltpu.make_async_copy(windows.at[member], mine_only, own_sem)
-    ours.start()
+    lane = lax.broadcasted_iota(jnp.int32, (R, 128), 1)
+
+    for part in range(2):
+
+        def take(block, unused):
+            chunk(part, block).wait()
+            place(part, block, other[part, block_rows(block), :].astype(jnp.int32), 1 - scan)
+            return unused
+
+        lax.fori_loop(0, BLOCKS, take, 0)
+
+        def give(strip, unused):
+            at_row = lax.broadcasted_iota(jnp.int32, (R, 128), 0) + (strip * R - delay)
+            inside = jnp.logical_and(at_row >= 0, at_row < W)
+            for position in range(G):
+                keep = lane < 128 - plan_ref[position, 2]
+                rows = pl.ds(plan_ref[position, 0] + (strip * R - delay + TOP), R)
+                rolled = [
+                    pltpu.roll(padded[part, plan_ref[position, 1] + j, rows, :], plan_ref[position, 3], 1) for j in range(3)
+                ]
+                for j in range(2):
+                    value = jnp.where(inside, jnp.where(keep, rolled[j], rolled[j + 1]), 0)
+                    windows[part, position, strip, :, 128 * j : 128 * j + 128] = value.astype(HELD)
+            trans[part, strip, mine] = windows[part, member, strip]
+            for step in range(1, G):
+                person = lax.rem(member + step, G)
+                pltpu.make_async_remote_copy(
+                    src_ref=windows.at[part, person, strip],
+                    dst_ref=trans.at[part, strip, mine],
+                    send_sem=trans_sent,
+                    recv_sem=trans_sem.at[part, strip],
+                    device_id=at(group, person),
+                    device_id_type=MESH,
+                ).start()
+            return unused
+
+        lax.fori_loop(0, S, give, 0)
 
     @pl.when(top)
     def _():
-        exits = pltpu.make_async_copy(exit_ref.at[member], inbox.at[:, 0:W, :], exit_sem)
-        exits.start()
         exits.wait()
 
-    ours.wait()
-
-    def own(strip, unused):
-        trans[strip, mine] = mine_only[strip]
-        return unused
-
-    lax.fori_loop(0, S, own, 0)
-    lane = lax.broadcasted_iota(jnp.int32, (R, 128), 1)
     row = lax.broadcasted_iota(jnp.int32, (R, 128), 0)
 
     def send_spread(strip, order):
@@ -269,9 +211,9 @@
             landed = inbox.at[:, pl.ds(pl.multiple_of(strip * R, R), R), :]
             pltpu.make_async_copy(landed, landed, in_sem.at[strip]).wait()
 
-        pltpu.make_async_copy(
-            trans.at[strip, 0 : G - 1], trans.at[strip, 0 : G - 1], trans_sem.at[strip]
-        ).wait()
+        for part in range(2):
+            come = trans.at[part, strip, 0 : G - 1]
+            pltpu.make_async_copy(come, come, trans_sem.at[part, strip]).wait()
         before = jnp.maximum(strip - 1, 0)
         at_strip = pl.multiple_of(strip * R, R)
         seen = pl.multiple_of(before * R, R)
@@ -288,8 +230,8 @@
                 cols = slice(128 * j, 128 * j + 128)
                 tall[order, 0, j, pl.ds(at_strip, R), :] = spread_re[j]
                 tall[order, 1, j, pl.ds(at_strip, R), :] = spread_im[j]
-                win_re = trans[strip, order, 0, :, cols].astype(jnp.int32).astype(jnp.float32)
-                win_im = trans[strip, order, 1, :, cols].astype(jnp.int32).astype(jnp.float32)
+                win_re = trans[0, strip, order, :, cols].astype(jnp.int32).astype(jnp.float32)
+                win_im = trans[1, strip, order, :, cols].astype(jnp.int32).astype(jnp.float32)
                 out_re = ((win_re * spread_re[j] + win_im * spread_im[j]) * (1.0 / FIX)).astype(jnp.bfloat16)
                 out_im = ((win_re * spread_im[j] - win_im * spread_re[j]) * (1.0 / FIX)).astype(jnp.bfloat16)
                 if order < G - 1:
@@ -343,7 +285,7 @@
 
         lax.fori_loop(0, S - 1, rest, 0)
 
-    pltpu.make_async_copy(windows.at[0 : G - 1], windows.at[0 : G - 1], trans_sent).wait()
+    pltpu.make_async_copy(windows.at[:, 0 : G - 1], windows.at[:, 0 : G - 1], trans_sent).wait()
     pltpu.make_async_copy(spr_ref.at[0 : G - 1], spr_ref.at[0 : G - 1], spr_sent).wait()
 
     @pl.when(group > 0)
@@ -353,23 +295,32 @@
     pltpu.make_async_copy(spr_ref.at[0 : G - 1], spr_ref.at[0 : G - 1], spr_sem).wait()
 
 
-def sweep(windows, exit_adjoint):
+def sweep(plan, amp, phase, exit_adjoint):
     return pl.pallas_call(
         sweep_kernel,
         out_shape=jax.ShapeDtypeStruct((G, S - 1, 2, R, W), jnp.bfloat16),
-        in_specs=[pl.BlockSpec(memory_space=pl.ANY)] * 2,
+        in_specs=[
+            pl.BlockSpec(memory_space=pltpu.SMEM),
+            pl.BlockSpec(memory_space=pltpu.VMEM),
+            pl.BlockSpec(memory_space=pltpu.VMEM),
+            pl.BlockSpec(memory_space=pl.ANY),
+        ],
         out_specs=pl.BlockSpec(memory_space=pltpu.VMEM),
         scratch_shapes=[
-            pltpu.VMEM((S, G, 2, R, W), HELD),
+            pltpu.VMEM((2, OBJ // 2, OBJ), HELD),
+            pltpu.VMEM((2, OBJ // 2, OBJ), HELD),
+            pltpu.VMEM((2, OBJ // 128 + 1, ROWS, 128), jnp.int32),
+            pltpu.VMEM((2, G, S, R, W), HELD),
+            pltpu.VMEM((2, S, G, R, W), HELD),
             pltpu.VMEM((2, S * R, W), jnp.bfloat16),
             pltpu.VMEM((S - 1, G, 2, R, W), jnp.bfloat16),
             pltpu.VMEM((S - 1, 2, R, W), jnp.bfloat16),
             pltpu.VMEM((G, 5, 2, 2, 8, 128), jnp.float32),
             pltpu.VMEM((G, 2, 2, S * R, 128), jnp.float32),
-            pltpu.VMEM((S, 2, R, W), HELD),
+            pltpu.SemaphoreType.DMA((2, BLOCKS)),
+            pltpu.SemaphoreType.DMA((2, BLOCKS)),
             pltpu.SemaphoreType.DMA,
-            pltpu.SemaphoreType.DMA,
-            pltpu.SemaphoreType.DMA((S,)),
+            pltpu.SemaphoreType.DMA((2, S)),
             pltpu.SemaphoreType.DMA((S - 1,)),
             pltpu.SemaphoreType.DMA,
             pltpu.SemaphoreType.DMA,
@@ -378,7 +329,7 @@
         ],
         compiler_params=pltpu.CompilerParams(collective_id=0, has_side_effects=True),
         name="sweep",
-    )(windows, exit_adjoint)
+    )(plan, amp, phase, exit_adjoint)
 
 
 def gather_kernel(other, offs_ref, fwd_ref, spr_ref, grad_ref, acc):
@@ -451,8 +402,9 @@
 
 
 def on_device(obj_amp, obj_phase, forward_waves, exit_adjoint, offsets):
-    half, other = swap(obj_amp[0], obj_phase[0])
-    spread = sweep(extract(offsets, half, other), exit_adjoint)
+    column, over = offsets[:, 1] // 128, offsets[:, 1] % 128
+    plan = jnp.stack([offsets[:, 0], column, over, (128 - over) % 128], axis=1)
+    spread = sweep(plan, obj_amp[0], obj_phase[0], exit_adjoint)
     leave = gather(offsets, forward_waves[0], spread, True)
     come = lax.ppermute(leave, "scan", [(0, 1), (1, 0)])
     keep = gather(offsets, forward_waves[0], spread, False)

time: 124 us -> 120 us (0.968)
  Pallas kernels: 111 us -> 107 us
    pallas_call x2 -> x0, Pallas kernels: 23.4 us -> none  [the longest x1 17.7 us: swap(): pl.pallas_call(swap_kernel, out_shape=(rows, rows), in_specs=[pl.BlockSpe...]
    pallas_call x1, Pallas kernels: 75.8 us -> 95.9 us  [sweep(): pl.pallas_call(sweep_kernel, out_shape=jax.ShapeDtypeStruct((G, S - 1, 2,...]
  transfers between devices with their start and end apart: 1 -> 1, of which waited for: 1 -> 1; matrix products, arithmetic and copies ran while one was open for 0% -> 0% of each run, Pallas kernels for 4% -> 5%
where the time goes in v5:
time: 120 us
  Pallas kernels  107 us (89%)
  waiting for transfers between devices  6.84 us (6%)
  other arithmetic  3.21 us (3%)
  starting transfers between devices  2.07 us (2%)
    pallas_call x1, Pallas kernels, sweep(): pl.pallas_call(sweep_kernel, out_shape=jax.ShapeDtypeStruct((G, S - 1, 2,...  95.9 us
    pallas_call x2, Pallas kernels, gather(): pl.pallas_call(functools.partial(gather_kernel, other), out_shape=jax.Sha...  11.1 us
    ppermute x1, waiting for transfers between devices, on_device(): come = lax.ppermute(leave, 'scan', [(0, 1), (1, 0)])  6.84 us
  transfers between devices with their start and end apart: 1, of which 1 were waited for; matrix products, arithmetic and copies ran while one was open for 0% of the time, Pallas kernels for 5%

profile of v5, /device:TPU:0, one launch (start us, length us, event | category | flops | bytes accessed | tf_op | source)
XLA Modules:
  0.0 119.9 jit_solution(16758879492370323758)
XLA Ops:
  0.0 0.8 copy.8.offs_ref
  0.8 0.0 copy-start
  0.8 0.1 add_select_fusion.2
  0.8 0.1 add_select_fusion
  0.9 0.7 pad_add_fusion.plan_ref
  1.6 95.9 %sweep.1.spr_ref = bf16[8,16,2,16,256]{4,3,2,1,0:T(8,128)(2,1)} custom-call(s32[8,4]{1,0:T(8,128)} %pad_add_fusion.plan_ref, f32[256,512]{1,0:T(8,128)} %bitcast.7, f32[256,512]{1,0:T(8,128)} %bitcast.8, bf16[8,2,256,256]{3,2,1,0:T(8,128)(2,1)} %exit_ref.1), custom_call_target="tpu_custom_call" | custom-call | tf_op jit(solution)/shard_map/sweep/pallas_call | solution.py:299
  97.5 0.0 copy-done
  97.5 4.8 %gather_other.1 = bf16[2,256,512]{2,1,0:T(8,128)(2,1)} custom-call(s32[8,2]{1,0:T(8,128)} %copy-done, bf16[8,2,256,256]{3,2,1,0:T(8,128)(2,1)} %bitcast.5, bf16[8,16,2,16,256]{4,3,2,1,0:T(8,128)(2,1)} %sweep.1.spr_ref), custom_call_target="tpu_custom_call" | custom-call | flops 20000000 | bytes 6000000 | tf_op jit(solution)/shard_map/gather_other/pallas_call | solution.py:389
  102.4 2.1 %collective-permute-start = (bf16[2,256,512]{2,1,0:T(8,128)(2,1)}, bf16[2,256,512]{2,1,0:T(8,128)(2,1)S(1)}, u32[]{:S(2)}, u32[]{:S(2)}) collective-permute-start(bf16[2,256,512]{2,1,0:T(8,128)(2,1)} %gather_other.1), channel_id=1, source_target_pairs={{0,1},{1,0},{2,3},{3,2},{4,5},{5,4},{6,7},{7,6},{8,9},{9,8},{10,11... | collective-permute-start | bytes 1572872 | tf_op jit(solution)/shard_map/ppermute | solution.py:409
  104.5 6.3 %gather_own.1 = f32[2,256,512]{2,1,0:T(8,128)} custom-call(s32[8,2]{1,0:T(8,128)} %copy-done, bf16[8,2,256,256]{3,2,1,0:T(8,128)(2,1)} %bitcast.6, bf16[8,16,2,16,256]{4,3,2,1,0:T(8,128)(2,1)} %sweep.1.spr_ref), custom_call_target="tpu_custom_call" | custom-call | flops 20000000 | bytes 6000000 | tf_op jit(solution)/shard_map/gather_own/pallas_call | solution.py:389
  110.7 6.8 %collective-permute-done = bf16[2,256,512]{2,1,0:T(8,128)(2,1)S(1)} collective-permute-done((bf16[2,256,512]{2,1,0:T(8,128)(2,1)}, bf16[2,256,512]{2,1,0:T(8,128)(2,1)S(1)}, u32[]{:S(2)}, u32[]{:S(2)}) %collective-permute-start) | collective-permute-done | bytes 524320 | tf_op jit(solution)/shard_map/ppermute | solution.py:409
  117.6 2.4 %add_bitcast_fusion = f32[1,2,256,512]{3,2,1,0:T(8,128)} fusion(f32[2,256,512]{2,1,0:T(8,128)} %gather_own.1, bf16[2,256,512]{2,1,0:T(8,128)(2,1)S(1)} %collective-permute-done), kind=kLoop, calls=%fused_computation | loop fusion | flops 524288 | bytes 2621440 | tf_op jit(solution)/shard_map/broadcast_in_dim | solution.py:411
Async XLA Ops:
  0.8 96.8 %copy-start = (s32[8,2]{1,0:T(8,128)}, s32[8,2]{1,0:T(8,128)S(1)}, u32[]{:S(2)}) copy-start(s32[8,2]{1,0:T(8,128)S(1)} %copy.8.offs_ref) | copy-start | bytes 196
  102.4 15.2 %collective-permute-start = (bf16[2,256,512]{2,1,0:T(8,128)(2,1)}, bf16[2,256,512]{2,1,0:T(8,128)(2,1)S(1)}, u32[]{:S(2)}, u32[]{:S(2)}) collective-permute-start(bf16[2,256,512]{2,1,0:T(8,128)(2,1)} %gather_other.1), channel_id=1, source_target_pairs={{0,1},{1,0},{2,3},{3,2},{4,5},{5,4},{6,7},{7,6},{8,9},{9,8},{10,11... | collective-permute-start | bytes 1572872 | tf_op jit(solution)/shard_map/ppermute | solution.py:409

commit v6 on v5

--- a/solution.py
+++ b/solution.py
@@ -20,6 +20,7 @@
 S = (W + SKEW) // R
 TOP = 16
 ROWS = OBJ + 40
+AHEAD = 7
 LATE = 5
 COLS = OBJ + 128
 FIX = 32767.0
@@ -153,18 +154,18 @@
     inbox[:, W:, :] = jnp.zeros((2, S * R - W, W), jnp.bfloat16)
     lane = lax.broadcasted_iota(jnp.int32, (R, 128), 1)
 
-    for part in range(2):
-
-        def take(block, unused):
+    def take(part):
+        def some_rows(block, unused):
             chunk(part, block).wait()
             place(part, block, other[part, block_rows(block), :].astype(jnp.int32), 1 - scan)
             return unused
 
-        lax.fori_loop(0, BLOCKS, take, 0)
-
-        def give(strip, unused):
-            at_row = lax.broadcasted_iota(jnp.int32, (R, 128), 0) + (strip * R - delay)
-            inside = jnp.logical_and(at_row >= 0, at_row < W)
+        lax.fori_loop(0, BLOCKS, some_rows, 0)
+
+    def give(strip, parts):
+        at_row = lax.broadcasted_iota(jnp.int32, (R, 128), 0) + (strip * R - delay)
+        inside = jnp.logical_and(at_row >= 0, at_row < W)
+        for part in parts:
             for position in range(G):
                 keep = lane < 128 - plan_ref[position, 2]
                 rows = pl.ds(plan_ref[position, 0] + (strip * R - delay + TOP), R)
@@ -185,9 +186,19 @@
                     device_id=at(group, person),
                     device_id_type=MESH,
                 ).start()
+
+    def gives(begin, end, parts):
+        def some_strips(strip, unused):
+            give(strip, parts)
             return unused
 
-        lax.fori_loop(0, S, give, 0)
+        lax.fori_loop(begin, end, some_strips, 0)
+
+    take(0)
+    gives(0, AHEAD, (0,))
+    take(1)
+    gives(0, AHEAD, (1,))
+    gives(AHEAD, S, (0, 1))
 
     @pl.when(top)
     def _():

time: 120 us -> 114 us (0.950)
  Pallas kernels: 107 us -> 99.8 us
    pallas_call x1, Pallas kernels: 95.9 us -> 88.6 us  [sweep(): pl.pallas_call(sweep_kernel, out_shape=jax.ShapeDtypeStruct((G, S - 1, 2,...]
where the time goes in v6:
time: 114 us; the launch traced here: 113 us
  Pallas kernels  99.8 us (88%)
  waiting for transfers between devices  7.59 us (7%)
  other arithmetic  3.21 us (3%)
  starting transfers between devices  2.01 us (2%)
    pallas_call x1, Pallas kernels, sweep(): pl.pallas_call(sweep_kernel, out_shape=jax.ShapeDtypeStruct((G, S - 1, 2,...  88.6 us
    pallas_call x2, Pallas kernels, gather(): pl.pallas_call(functools.partial(gather_kernel, other), out_shape=jax.Sha...  11.2 us
    ppermute x1, waiting for transfers between devices, on_device(): come = lax.ppermute(leave, 'scan', [(0, 1), (1, 0)])  7.59 us
    broadcast_in_dim x1, other arithmetic, on_device(): return (keep + come.astype(jnp.float32))[None]  2.37 us
  transfers between devices with their start and end apart: 1, of which 1 were waited for; matrix products, arithmetic and copies ran while one was open for 0% of the time, Pallas kernels for 5%

profile of v6, /device:TPU:0, one launch (start us, length us, event | category | flops | bytes accessed | tf_op | source)
XLA Modules:
  0.0 113.4 jit_solution(1889066459801167976)
XLA Ops:
  0.0 0.8 copy.8.offs_ref
  0.8 0.0 copy-start
  0.8 0.1 add_select_fusion.2
  0.8 0.1 add_select_fusion
  0.9 0.7 pad_add_fusion.plan_ref
  1.6 88.6 %sweep.1.spr_ref = bf16[8,16,2,16,256]{4,3,2,1,0:T(8,128)(2,1)} custom-call(s32[8,4]{1,0:T(8,128)} %pad_add_fusion.plan_ref, f32[256,512]{1,0:T(8,128)} %bitcast.7, f32[256,512]{1,0:T(8,128)} %bitcast.8, bf16[8,2,256,256]{3,2,1,0:T(8,128)(2,1)} %exit_ref.1), custom_call_target="tpu_custom_call" | custom-call | tf_op jit(solution)/shard_map/sweep/pallas_call | solution.py:310
  90.2 0.0 copy-done
  90.3 5.7 %gather_other.1 = bf16[2,256,512]{2,1,0:T(8,128)(2,1)} custom-call(s32[8,2]{1,0:T(8,128)} %copy-done, bf16[8,2,256,256]{3,2,1,0:T(8,128)(2,1)} %bitcast.5, bf16[8,16,2,16,256]{4,3,2,1,0:T(8,128)(2,1)} %sweep.1.spr_ref), custom_call_target="tpu_custom_call" | custom-call | flops 20000000 | bytes 6000000 | tf_op jit(solution)/shard_map/gather_other/pallas_call | solution.py:400
  95.9 2.0 %collective-permute-start = (bf16[2,256,512]{2,1,0:T(8,128)(2,1)}, bf16[2,256,512]{2,1,0:T(8,128)(2,1)S(1)}, u32[]{:S(2)}, u32[]{:S(2)}) collective-permute-start(bf16[2,256,512]{2,1,0:T(8,128)(2,1)} %gather_other.1), channel_id=1, source_target_pairs={{0,1},{1,0},{2,3},{3,2},{4,5},{5,4},{6,7},{7,6},{8,9},{9,8},{10,11... | collective-permute-start | bytes 1572872 | tf_op jit(solution)/shard_map/ppermute | solution.py:420
  97.9 5.5 %gather_own.1 = f32[2,256,512]{2,1,0:T(8,128)} custom-call(s32[8,2]{1,0:T(8,128)} %copy-done, bf16[8,2,256,256]{3,2,1,0:T(8,128)(2,1)} %bitcast.6, bf16[8,16,2,16,256]{4,3,2,1,0:T(8,128)(2,1)} %sweep.1.spr_ref), custom_call_target="tpu_custom_call" | custom-call | flops 20000000 | bytes 6000000 | tf_op jit(solution)/shard_map/gather_own/pallas_call | solution.py:400
  103.5 7.6 %collective-permute-done = bf16[2,256,512]{2,1,0:T(8,128)(2,1)S(1)} collective-permute-done((bf16[2,256,512]{2,1,0:T(8,128)(2,1)}, bf16[2,256,512]{2,1,0:T(8,128)(2,1)S(1)}, u32[]{:S(2)}, u32[]{:S(2)}) %collective-permute-start) | collective-permute-done | bytes 524320 | tf_op jit(solution)/shard_map/ppermute | solution.py:420
  111.1 2.4 %add_bitcast_fusion = f32[1,2,256,512]{3,2,1,0:T(8,128)} fusion(f32[2,256,512]{2,1,0:T(8,128)} %gather_own.1, bf16[2,256,512]{2,1,0:T(8,128)(2,1)S(1)} %collective-permute-done), kind=kLoop, calls=%fused_computation | loop fusion | flops 524288 | bytes 2621440 | tf_op jit(solution)/shard_map/broadcast_in_dim | solution.py:422
Async XLA Ops:
  0.8 89.5 %copy-start = (s32[8,2]{1,0:T(8,128)}, s32[8,2]{1,0:T(8,128)S(1)}, u32[]{:S(2)}) copy-start(s32[8,2]{1,0:T(8,128)S(1)} %copy.8.offs_ref) | copy-start | bytes 196
  95.9 15.1 %collective-permute-start = (bf16[2,256,512]{2,1,0:T(8,128)(2,1)}, bf16[2,256,512]{2,1,0:T(8,128)(2,1)S(1)}, u32[]{:S(2)}, u32[]{:S(2)}) collective-permute-start(bf16[2,256,512]{2,1,0:T(8,128)(2,1)} %gather_other.1), channel_id=1, source_target_pairs={{0,1},{1,0},{2,3},{3,2},{4,5},{5,4},{6,7},{7,6},{8,9},{9,8},{10,11... | collective-permute-start | bytes 1572872 | tf_op jit(solution)/shard_map/ppermute | solution.py:420

commit v7 on v6

--- a/solution.py
+++ b/solution.py
@@ -84,8 +84,8 @@
 
 
 def sweep_kernel(
-    plan_ref, amp_ref, phase_ref, exit_ref, spr_ref, half, other, padded, windows, trans, inbox, spread_out, wave_out, waves, tall,
-    half_sem, half_sent, exit_sem, trans_sem, in_sem, spr_sem, trans_sent, spr_sent, wave_sent,
+    plan_ref, amp_hbm, phase_hbm, exit_ref, spr_ref, amp_ref, phase_ref, half, other, padded, windows, trans, inbox, spread_out, wave_out, waves, tall,
+    amp_sem, phase_sem, half_sem, half_sent, exit_sem, trans_sem, in_sem, spr_sem, trans_sent, spr_sent, wave_sent,
 ):
     sec = lax.axis_index("sec")
     scan = lax.axis_index("scan")
@@ -97,6 +97,12 @@
     def at(g, m):
         return (g * G + m, scan)
 
+    loads = (
+        pltpu.make_async_copy(amp_hbm, amp_ref, amp_sem),
+        pltpu.make_async_copy(phase_hbm, phase_ref, phase_sem),
+    )
+    for load in loads:
+        load.start()
     barrier = pltpu.get_barrier_semaphore()
     for step in range(1, G):
         pl.semaphore_signal(barrier, 1, device_id=at(group, lax.rem(member + step, G)), device_id_type=MESH)
@@ -138,6 +144,9 @@
         to = pl.ds(pl.multiple_of(TOP + owner * (OBJ // 2) + block * BLOCK, 8), BLOCK)
         for j in range(OBJ // 128):
             padded[part, j, to, :] = value[:, 128 * j : 128 * j + 128]
+
+    for load in loads:
+        load.wait()
 
     for part, wave in enumerate((jnp.cos, jnp.sin)):
 
@@ -309,15 +318,17 @@
 def sweep(plan, amp, phase, exit_adjoint):
     return pl.pallas_call(
         sweep_kernel,
-        out_shape=jax.ShapeDtypeStruct((G, S - 1, 2, R, W), jnp.bfloat16),
+        out_shape=pltpu.VMEM((G, S - 1, 2, R, W), jnp.bfloat16),
         in_specs=[
             pl.BlockSpec(memory_space=pltpu.SMEM),
-            pl.BlockSpec(memory_space=pltpu.VMEM),
-            pl.BlockSpec(memory_space=pltpu.VMEM),
+            pl.BlockSpec(memory_space=pl.ANY),
+            pl.BlockSpec(memory_space=pl.ANY),
             pl.BlockSpec(memory_space=pl.ANY),
         ],
         out_specs=pl.BlockSpec(memory_space=pltpu.VMEM),
         scratch_shapes=[
+            pltpu.VMEM((OBJ // 2, OBJ), jnp.float32),
+            pltpu.VMEM((OBJ // 2, OBJ), jnp.float32),
             pltpu.VMEM((2, OBJ // 2, OBJ), HELD),
             pltpu.VMEM((2, OBJ // 2, OBJ), HELD),
             pltpu.VMEM((2, OBJ // 128 + 1, ROWS, 128), jnp.int32),
@@ -328,6 +339,8 @@
             pltpu.VMEM((S - 1, 2, R, W), jnp.bfloat16),
             pltpu.VMEM((G, 5, 2, 2, 8, 128), jnp.float32),
             pltpu.VMEM((G, 2, 2, S * R, 128), jnp.float32),
+            pltpu.SemaphoreType.DMA,
+            pltpu.SemaphoreType.DMA,
             pltpu.SemaphoreType.DMA((2, BLOCKS)),
             pltpu.SemaphoreType.DMA((2, BLOCKS)),
             pltpu.SemaphoreType.DMA,
@@ -338,7 +351,7 @@
             pltpu.SemaphoreType.DMA,
             pltpu.SemaphoreType.DMA,
         ],
-        compiler_params=pltpu.CompilerParams(collective_id=0, has_side_effects=True),
+        compiler_params=pltpu.CompilerParams(collective_id=0, has_side_effects=True, vmem_limit_bytes=62_390_272),
         name="sweep",
     )(plan, amp, phase, exit_adjoint)
 
@@ -407,6 +420,7 @@
         ],
         out_specs=pl.BlockSpec(memory_space=pltpu.VMEM),
         scratch_shapes=[pltpu.VMEM((2, OBJ // 128 + 1, OBJ // 2 + 2 * RUN, 128), jnp.float32)],
+        compiler_params=pltpu.CompilerParams(vmem_limit_bytes=16 << 20),
         cost_estimate=pl.CostEstimate(flops=20_000_000, bytes_accessed=6_000_000, transcendentals=0),
         name="gather_other" if other else "gather_own",
     )(offsets, forward, spread)
@@ -416,9 +430,11 @@
     column, over = offsets[:, 1] // 128, offsets[:, 1] % 128
     plan = jnp.stack([offsets[:, 0], column, over, (128 - over) % 128], axis=1)
     spread = sweep(plan, obj_amp[0], obj_phase[0], exit_adjoint)
-    leave = gather(offsets, forward_waves[0], spread, True)
+    spread = pltpu.with_memory_space_constraint(spread, pltpu.VMEM)
+    forward = pltpu.with_memory_space_constraint(forward_waves[0], pltpu.VMEM)
+    leave = gather(offsets, forward, spread, True)
     come = lax.ppermute(leave, "scan", [(0, 1), (1, 0)])
-    keep = gather(offsets, forward_waves[0], spread, False)
+    keep = gather(offsets, forward, spread, False)
     return (keep + come.astype(jnp.float32))[None]
 
 

time: 114 us -> 108 us (0.947)
  Pallas kernels: 99.8 us -> 93.2 us
  waiting for transfers between devices: 7.59 us -> 10.2 us
  other arithmetic: 3.21 us -> 1.98 us
    pallas_call x2, Pallas kernels: 11.2 us -> 6.26 us  [gather(): pl.pallas_call(functools.partial(gather_kernel, other), out_shape=jax.Sha...]
    ppermute x1, waiting for transfers between devices: 7.59 us -> 10.2 us  [on_device(): come = lax.ppermute(leave, 'scan', [(0, 1), (1, 0)])]
    pallas_call x1, Pallas kernels: 88.6 us -> 87 us  [sweep(): pl.pallas_call(sweep_kernel, out_shape=pltpu.VMEM((G, S - 1, 2, R, W), jn...]
    broadcast_in_dim x1, other arithmetic: 2.37 us -> 1.14 us  [on_device(): return (keep + come.astype(jnp.float32))[None]]
  transfers between devices with their start and end apart: 1 -> 1, of which waited for: 1 -> 1; matrix products, arithmetic and copies ran while one was open for 0% -> 0% of each run, Pallas kernels for 5% -> 3%
where the time goes in v7:
time: 108 us
  Pallas kernels  93.2 us (86%)
  waiting for transfers between devices  10.2 us (9%)
  other arithmetic  1.98 us (2%)
  starting transfers between devices  1.78 us (2%)
    pallas_call x1, Pallas kernels, sweep(): pl.pallas_call(sweep_kernel, out_shape=pltpu.VMEM((G, S - 1, 2, R, W), jn...  87 us
    ppermute x1, waiting for transfers between devices, on_device(): come = lax.ppermute(leave, 'scan', [(0, 1), (1, 0)])  10.2 us
    pallas_call x2, Pallas kernels, gather(): pl.pallas_call(functools.partial(gather_kernel, other), out_shape=jax.Sha...  6.26 us
  transfers between devices with their start and end apart: 1, of which 1 were waited for; matrix products, arithmetic and copies ran while one was open for 0% of the time, Pallas kernels for 3%

profile of v7, /device:TPU:0, one launch (start us, length us, event | category | flops | bytes accessed | tf_op | source)
XLA Modules:
  0.0 108.0 jit_solution(11606500275915824421)
XLA Ops:
  0.0 0.8 copy.8.offs_ref
  0.8 0.1 add_select_fusion.2
  0.8 0.1 add_select_fusion
  0.9 0.7 pad_add_fusion.plan_ref
  1.6 0.0 copy-start
  1.6 87.0 %sweep.1.spr_ref = bf16[8,16,2,16,256]{4,3,2,1,0:T(8,128)(2,1)S(1)} custom-call(s32[8,4]{1,0:T(8,128)} %pad_add_fusion.plan_ref, f32[256,512]{1,0:T(8,128)} %bitcast.7, f32[256,512]{1,0:T(8,128)} %bitcast.8, bf16[8,2,256,256]{3,2,1,0:T(8,128)(2,1)} %exit_ref.1), custom_call_target="tpu_custom_call" | custom-call | tf_op jit(solution)/shard_map/sweep/pallas_call | solution.py:319
  88.6 0.0 copy-done
  88.6 3.2 %gather_other.1 = bf16[2,256,512]{2,1,0:T(8,128)(2,1)S(1)} custom-call(s32[8,2]{1,0:T(8,128)S(1)} %copy.8.offs_ref, bf16[8,2,256,256]{3,2,1,0:T(8,128)(2,1)S(1)} %bitcast.5, bf16[8,16,2,16,256]{4,3,2,1,0:T(8,128)(2,1)S(1)} %sweep.1.spr_ref), custom_call_target="tpu_custom_call" | custom-call | flops 20000000 | bytes 6000000 | tf_op jit(solution)/shard_map/gather_other/pallas_call | solution.py:413
  91.8 1.8 %collective-permute-start = (bf16[2,256,512]{2,1,0:T(8,128)(2,1)S(1)}, bf16[2,256,512]{2,1,0:T(8,128)(2,1)S(1)}, u32[]{:S(2)}, u32[]{:S(2)}) collective-permute-start(bf16[2,256,512]{2,1,0:T(8,128)(2,1)S(1)} %gather_other.1), channel_id=1, source_target_pairs={{0,1},{1,0},{2,3},{3,2},{4,5},{5,4},{6,7},{7,6},{8,9},{9,8},{10,11... | collective-permute-start | bytes 1572872 | tf_op jit(solution)/shard_map/ppermute | solution.py:436
  93.6 3.0 %gather_own.1 = f32[2,256,512]{2,1,0:T(8,128)S(1)} custom-call(s32[8,2]{1,0:T(8,128)S(1)} %copy.8.offs_ref, bf16[8,2,256,256]{3,2,1,0:T(8,128)(2,1)S(1)} %bitcast.6, bf16[8,16,2,16,256]{4,3,2,1,0:T(8,128)(2,1)S(1)} %sweep.1.spr_ref), custom_call_target="tpu_custom_call" | custom-call | flops 20000000 | bytes 6000000 | tf_op jit(solution)/shard_map/gather_own/pallas_call | solution.py:413
  96.6 10.2 %collective-permute-done = bf16[2,256,512]{2,1,0:T(8,128)(2,1)S(1)} collective-permute-done((bf16[2,256,512]{2,1,0:T(8,128)(2,1)S(1)}, bf16[2,256,512]{2,1,0:T(8,128)(2,1)S(1)}, u32[]{:S(2)}, u32[]{:S(2)}) %collective-permute-start) | collective-permute-done | bytes 524320 | tf_op jit(solution)/shard_map/ppermute | solution.py:436
  106.8 1.1 %add_bitcast_fusion = f32[1,2,256,512]{3,2,1,0:T(8,128)} fusion(f32[2,256,512]{2,1,0:T(8,128)S(1)} %gather_own.1, bf16[2,256,512]{2,1,0:T(8,128)(2,1)S(1)} %collective-permute-done), kind=kLoop, calls=%fused_computation | loop fusion | flops 524288 | bytes 2621440 | tf_op jit(solution)/shard_map/broadcast_in_dim | solution.py:438
Async XLA Ops:
  1.6 87.0 %copy-start = (bf16[1,8,2,256,256]{4,3,2,1,0:T(8,128)(2,1)S(1)}, bf16[1,8,2,256,256]{4,3,2,1,0:T(8,128)(2,1)}, u32[]{:S(2)}) copy-start(bf16[1,8,2,256,256]{4,3,2,1,0:T(8,128)(2,1)} %param.7) | copy-start | bytes 6291460
  91.8 15.0 %collective-permute-start = (bf16[2,256,512]{2,1,0:T(8,128)(2,1)S(1)}, bf16[2,256,512]{2,1,0:T(8,128)(2,1)S(1)}, u32[]{:S(2)}, u32[]{:S(2)}) collective-permute-start(bf16[2,256,512]{2,1,0:T(8,128)(2,1)S(1)} %gather_other.1), channel_id=1, source_target_pairs={{0,1},{1,0},{2,3},{3,2},{4,5},{5,4},{6,7},{7,6},{8,9},{9,8},{10,11... | collective-permute-start | bytes 1572872 | tf_op jit(solution)/shard_map/ppermute | solution.py:436

commit v8 on v7

--- a/solution.py
+++ b/solution.py
@@ -84,7 +84,7 @@
 
 
 def sweep_kernel(
-    plan_ref, amp_hbm, phase_hbm, exit_ref, spr_ref, amp_ref, phase_ref, half, other, padded, windows, trans, inbox, spread_out, wave_out, waves, tall,
+    offs_ref, amp_hbm, phase_hbm, exit_ref, spr_ref, amp_ref, phase_ref, half, other, padded, windows, trans, inbox, spread_out, wave_out, waves, tall,
     amp_sem, phase_sem, half_sem, half_sent, exit_sem, trans_sem, in_sem, spr_sem, trans_sent, spr_sent, wave_sent,
 ):
     sec = lax.axis_index("sec")
@@ -176,11 +176,12 @@
         inside = jnp.logical_and(at_row >= 0, at_row < W)
         for part in parts:
             for position in range(G):
-                keep = lane < 128 - plan_ref[position, 2]
-                rows = pl.ds(plan_ref[position, 0] + (strip * R - delay + TOP), R)
-                rolled = [
-                    pltpu.roll(padded[part, plan_ref[position, 1] + j, rows, :], plan_ref[position, 3], 1) for j in range(3)
-                ]
+                column = lax.shift_right_logical(offs_ref[position, 1], 7)
+                over = lax.bitwise_and(offs_ref[position, 1], 127)
+                turn = lax.bitwise_and(128 - over, 127)
+                keep = lane < 128 - over
+                rows = pl.ds(offs_ref[position, 0] + (strip * R - delay + TOP), R)
+                rolled = [pltpu.roll(padded[part, column + j, rows, :], turn, 1) for j in range(3)]
                 for j in range(2):
                     value = jnp.where(inside, jnp.where(keep, rolled[j], rolled[j + 1]), 0)
                     windows[part, position, strip, :, 128 * j : 128 * j + 128] = value.astype(HELD)
@@ -315,7 +316,7 @@
     pltpu.make_async_copy(spr_ref.at[0 : G - 1], spr_ref.at[0 : G - 1], spr_sem).wait()
 
 
-def sweep(plan, amp, phase, exit_adjoint):
+def sweep(offsets, amp, phase, exit_adjoint):
     return pl.pallas_call(
         sweep_kernel,
         out_shape=pltpu.VMEM((G, S - 1, 2, R, W), jnp.bfloat16),
@@ -353,7 +354,7 @@
         ],
         compiler_params=pltpu.CompilerParams(collective_id=0, has_side_effects=True, vmem_limit_bytes=62_390_272),
         name="sweep",
-    )(plan, amp, phase, exit_adjoint)
+    )(offsets, amp, phase, exit_adjoint)
 
 
 def gather_kernel(other, offs_ref, fwd_ref, spr_ref, grad_ref, acc):
@@ -427,9 +428,7 @@
 
 
 def on_device(obj_amp, obj_phase, forward_waves, exit_adjoint, offsets):
-    column, over = offsets[:, 1] // 128, offsets[:, 1] % 128
-    plan = jnp.stack([offsets[:, 0], column, over, (128 - over) % 128], axis=1)
-    spread = sweep(plan, obj_amp[0], obj_phase[0], exit_adjoint)
+    spread = sweep(offsets, obj_amp[0], obj_phase[0], exit_adjoint)
     spread = pltpu.with_memory_space_constraint(spread, pltpu.VMEM)
     forward = pltpu.with_memory_space_constraint(forward_waves[0], pltpu.VMEM)
     leave = gather(offsets, forward, spread, True)

time: 108 us -> 108 us (level)
  waiting for transfers between devices: 10.2 us -> 8.29 us
  starting transfers between devices: 1.78 us -> 3.66 us
    ppermute x1, waiting for transfers between devices: 10.2 us -> 8.29 us  [on_device(): come = lax.ppermute(leave, 'scan', [(0, 1), (1, 0)])]
    ppermute x1, starting transfers between devices: 1.78 us -> 3.66 us  [on_device(): come = lax.ppermute(leave, 'scan', [(0, 1), (1, 0)])]
where the time goes in v8:
time: 108 us
  Pallas kernels  93.3 us (86%)
  waiting for transfers between devices  8.29 us (8%)
  starting transfers between devices  3.66 us (3%)
  local copies, waits for them, and re-layouts  1.35 us (1%)
  other arithmetic  1.13 us (1%)
    pallas_call x1, Pallas kernels, sweep(): pl.pallas_call(sweep_kernel, out_shape=pltpu.VMEM((G, S - 1, 2, R, W), jn...  87 us
    ppermute x1, waiting for transfers between devices, on_device(): come = lax.ppermute(leave, 'scan', [(0, 1), (1, 0)])  8.29 us
    pallas_call x2, Pallas kernels, gather(): pl.pallas_call(functools.partial(gather_kernel, other), out_shape=jax.Sha...  6.26 us
    ppermute x1, starting transfers between devices, on_device(): come = lax.ppermute(leave, 'scan', [(0, 1), (1, 0)])  3.66 us
  transfers between devices with their start and end apart: 1, of which 1 were waited for; matrix products, arithmetic and copies ran while one was open for 0% of the time, Pallas kernels for 3%

profile of v8, /device:TPU:0, one launch (start us, length us, event | category | flops | bytes accessed | tf_op | source)
XLA Modules:
  0.0 107.7 jit_solution(4094300449978103454)
XLA Ops:
  0.0 1.3 %copy.7.offs_ref = s32[8,2]{1,0:T(8,128)} copy(s32[8,2]{0,1:T(2,128)} %param.9) | data formatting | bytes 128 | tf_op args[4]
  1.3 0.0 copy-start
  1.3 0.0 copy-start.1
  1.3 87.0 %sweep.1.spr_ref = bf16[8,16,2,16,256]{4,3,2,1,0:T(8,128)(2,1)S(1)} custom-call(s32[8,2]{1,0:T(8,128)} %copy.7.offs_ref, f32[256,512]{1,0:T(8,128)} %bitcast.7, f32[256,512]{1,0:T(8,128)} %bitcast.8, bf16[8,2,256,256]{3,2,1,0:T(8,128)(2,1)} %exit_ref.1), custom_call_target="tpu_custom_call" | custom-call | tf_op jit(solution)/shard_map/sweep/pallas_call | solution.py:320
  88.3 0.0 copy-done
  88.4 0.0 copy-done.1
  88.4 2.7 %gather_other.1 = bf16[2,256,512]{2,1,0:T(8,128)(2,1)S(1)} custom-call(s32[8,2]{1,0:T(8,128)S(1)} %copy-done.1, bf16[8,2,256,256]{3,2,1,0:T(8,128)(2,1)S(1)} %bitcast.5, bf16[8,16,2,16,256]{4,3,2,1,0:T(8,128)(2,1)S(1)} %sweep.1.spr_ref), custom_call_target="tpu_custom_call" | custom-call | flops 20000000 | bytes 6000000 | tf_op jit(solution)/shard_map/gather_other/pallas_call | solution.py:414
  91.1 3.7 %collective-permute-start = (bf16[2,256,512]{2,1,0:T(8,128)(2,1)S(1)}, bf16[2,256,512]{2,1,0:T(8,128)(2,1)S(1)}, u32[]{:S(2)}, u32[]{:S(2)}) collective-permute-start(bf16[2,256,512]{2,1,0:T(8,128)(2,1)S(1)} %gather_other.1), channel_id=1, source_target_pairs={{0,1},{1,0},{2,3},{3,2},{4,5},{5,4},{6,7},{7,6},{8,9},{9,8},{10,11... | collective-permute-start | bytes 1572872 | tf_op jit(solution)/shard_map/ppermute | solution.py:435
  94.7 3.6 %gather_own.1 = f32[2,256,512]{2,1,0:T(8,128)S(1)} custom-call(s32[8,2]{1,0:T(8,128)S(1)} %copy-done.1, bf16[8,2,256,256]{3,2,1,0:T(8,128)(2,1)S(1)} %bitcast.6, bf16[8,16,2,16,256]{4,3,2,1,0:T(8,128)(2,1)S(1)} %sweep.1.spr_ref), custom_call_target="tpu_custom_call" | custom-call | flops 20000000 | bytes 6000000 | tf_op jit(solution)/shard_map/gather_own/pallas_call | solution.py:414
  98.3 8.3 %collective-permute-done = bf16[2,256,512]{2,1,0:T(8,128)(2,1)S(1)} collective-permute-done((bf16[2,256,512]{2,1,0:T(8,128)(2,1)S(1)}, bf16[2,256,512]{2,1,0:T(8,128)(2,1)S(1)}, u32[]{:S(2)}, u32[]{:S(2)}) %collective-permute-start) | collective-permute-done | bytes 524320 | tf_op jit(solution)/shard_map/ppermute | solution.py:435
  106.6 1.1 %add_bitcast_fusion = f32[1,2,256,512]{3,2,1,0:T(8,128)} fusion(f32[2,256,512]{2,1,0:T(8,128)S(1)} %gather_own.1, bf16[2,256,512]{2,1,0:T(8,128)(2,1)S(1)} %collective-permute-done), kind=kLoop, calls=%fused_computation | loop fusion | flops 524288 | bytes 2621440 | tf_op jit(solution)/shard_map/broadcast_in_dim | solution.py:437
Async XLA Ops:
  1.3 87.0 %copy-start = (bf16[1,8,2,256,256]{4,3,2,1,0:T(8,128)(2,1)S(1)}, bf16[1,8,2,256,256]{4,3,2,1,0:T(8,128)(2,1)}, u32[]{:S(2)}) copy-start(bf16[1,8,2,256,256]{4,3,2,1,0:T(8,128)(2,1)} %param.7) | copy-start | bytes 6291460
  1.3 87.0 %copy-start.1 = (s32[8,2]{1,0:T(8,128)S(1)}, s32[8,2]{1,0:T(8,128)}, u32[]{:S(2)}) copy-start(s32[8,2]{1,0:T(8,128)} %copy.7.offs_ref) | copy-start | bytes 196
  91.1 15.5 %collective-permute-start = (bf16[2,256,512]{2,1,0:T(8,128)(2,1)S(1)}, bf16[2,256,512]{2,1,0:T(8,128)(2,1)S(1)}, u32[]{:S(2)}, u32[]{:S(2)}) collective-permute-start(bf16[2,256,512]{2,1,0:T(8,128)(2,1)S(1)} %gather_other.1), channel_id=1, source_target_pairs={{0,1},{1,0},{2,3},{3,2},{4,5},{5,4},{6,7},{7,6},{8,9},{9,8},{10,11... | collective-permute-start | bytes 1572872 | tf_op jit(solution)/shard_map/ppermute | solution.py:435

commit v9 on v8

--- a/solution.py
+++ b/solution.py
@@ -25,7 +25,7 @@
 COLS = OBJ + 128
 FIX = 32767.0
 HELD = jnp.int16
-RUN = 64
+RUN = 128
 BLOCK = 32
 BLOCKS = OBJ // 2 // BLOCK
 
@@ -357,7 +357,7 @@
     )(offsets, amp, phase, exit_adjoint)
 
 
-def gather_kernel(other, offs_ref, fwd_ref, spr_ref, grad_ref, acc):
+def gather_kernel(other, parts, offs_ref, fwd_ref, spr_ref, grad_ref, acc):
     scan = lax.axis_index("scan")
     start = ((1 - scan) if other else scan) * (OBJ // 2)
     acc[...] = jnp.zeros_like(acc)
@@ -387,8 +387,9 @@
                 spread_re, spread_im = (part.astype(jnp.float32) for part in spread)
                 terms[0].append(pltpu.roll(fwd_re * spread_re + fwd_im * spread_im, over, 1))
                 terms[1].append(pltpu.roll(fwd_re * spread_im - fwd_im * spread_re, over, 1))
-            for part in range(2):
+            for part in parts:
                 near, far = terms[part]
+                part = part - parts[0]
                 acc[part, column, to, :] += jnp.where(keep, near, 0.0)
                 acc[part, column + 1, to, :] += jnp.where(keep, far, near)
                 acc[part, column + 2, to, :] += jnp.where(keep, 0.0, far)
@@ -402,7 +403,7 @@
     def split(block, unused):
         rows = pl.ds(pl.multiple_of(block * BLOCK, BLOCK), BLOCK)
         source = pl.ds(pl.multiple_of(RUN + block * BLOCK, BLOCK), BLOCK)
-        for part in range(2):
+        for part in range(len(parts)):
             for j in range(OBJ // 128):
                 grad_ref[part, rows, 128 * j : 128 * j + 128] = acc[part, j, source, :].astype(grad_ref.dtype)
         return unused
@@ -410,17 +411,17 @@
     lax.fori_loop(0, BLOCKS, split, 0)
 
 
-def gather(offsets, forward, spread, other):
+def gather(offsets, forward, spread, other, parts):
     return pl.pallas_call(
-        functools.partial(gather_kernel, other),
-        out_shape=jax.ShapeDtypeStruct((2, OBJ // 2, OBJ), jnp.bfloat16 if other else jnp.float32),
+        functools.partial(gather_kernel, other, parts),
+        out_shape=jax.ShapeDtypeStruct((len(parts), OBJ // 2, OBJ), jnp.bfloat16 if other else jnp.float32),
         in_specs=[
             pl.BlockSpec(memory_space=pltpu.SMEM),
             pl.BlockSpec(memory_space=pltpu.VMEM),
             pl.BlockSpec(memory_space=pltpu.VMEM),
         ],
         out_specs=pl.BlockSpec(memory_space=pltpu.VMEM),
-        scratch_shapes=[pltpu.VMEM((2, OBJ // 128 + 1, OBJ // 2 + 2 * RUN, 128), jnp.float32)],
+        scratch_shapes=[pltpu.VMEM((len(parts), OBJ // 128 + 1, OBJ // 2 + 2 * RUN, 128), jnp.float32)],
         compiler_params=pltpu.CompilerParams(vmem_limit_bytes=16 << 20),
         cost_estimate=pl.CostEstimate(flops=20_000_000, bytes_accessed=6_000_000, transcendentals=0),
         name="gather_other" if other else "gather_own",
@@ -431,10 +432,11 @@
     spread = sweep(offsets, obj_amp[0], obj_phase[0], exit_adjoint)
     spread = pltpu.with_memory_space_constraint(spread, pltpu.VMEM)
     forward = pltpu.with_memory_space_constraint(forward_waves[0], pltpu.VMEM)
-    leave = gather(offsets, forward, spread, True)
-    come = lax.ppermute(leave, "scan", [(0, 1), (1, 0)])
-    keep = gather(offsets, forward, spread, False)
-    return (keep + come.astype(jnp.float32))[None]
+    come = [
+        lax.ppermute(gather(offsets, forward, spread, True, (part,)), "scan", [(0, 1), (1, 0)]) for part in range(2)
+    ]
+    keep = gather(offsets, forward, spread, False, (0, 1))
+    return (keep + jnp.concatenate(come).astype(jnp.float32))[None]
 
 
 def solution(mesh):

time: 108 us -> 107 us (level)
  waiting for transfers between devices: 8.29 us -> 6.4 us
    ppermute x1 -> x2, waiting for transfers between devices: 8.29 us -> 6.4 us  [on_device(): lax.ppermute(gather(offsets, forward, spread, True, (part,)), 'scan', [(0...]
    pallas_call x2 -> x3, Pallas kernels: 6.26 us -> 7.01 us  [gather(): pl.pallas_call(functools.partial(gather_kernel, other, parts), out_shape=...]
    ppermute x1 -> x2, starting transfers between devices: 3.66 us -> 3.69 us  [on_device(): lax.ppermute(gather(offsets, forward, spread, True, (part,)), 'scan', [(0...]
  transfers between devices with their start and end apart: 1 -> 2, of which waited for: 1 -> 2; matrix products, arithmetic and copies ran while one was open for 0% -> 0% of each run, Pallas kernels for 3% -> 5%
where the time goes in v9:
time: 107 us
  Pallas kernels  94 us (88%)
  waiting for transfers between devices  6.4 us (6%)
  starting transfers between devices  3.69 us (3%)
  local copies, waits for them, and re-layouts  1.35 us (1%)
  other arithmetic  1.13 us (1%)
    pallas_call x1, Pallas kernels, sweep(): pl.pallas_call(sweep_kernel, out_shape=pltpu.VMEM((G, S - 1, 2, R, W), jn...  87 us
    pallas_call x3, Pallas kernels, gather(): pl.pallas_call(functools.partial(gather_kernel, other, parts), out_shape=...  7.01 us
    ppermute x2, waiting for transfers between devices, on_device(): lax.ppermute(gather(offsets, forward, spread, True, (part,)), 'scan', [(0...  6.4 us
    ppermute x2, starting transfers between devices, on_device(): lax.ppermute(gather(offsets, forward, spread, True, (part,)), 'scan', [(0...  3.69 us
  transfers between devices with their start and end apart: 2, of which 2 were waited for; matrix products, arithmetic and copies ran while one was open for 0% of the time, Pallas kernels for 5%

profile of v9, /device:TPU:0, one launch (start us, length us, event | category | flops | bytes accessed | tf_op | source)
XLA Modules:
  0.0 106.6 jit_solution(1344033377161089711)
XLA Ops:
  0.0 1.3 %copy.7.offs_ref = s32[8,2]{1,0:T(8,128)} copy(s32[8,2]{0,1:T(2,128)} %param.9) | data formatting | bytes 128 | tf_op args[4]
  1.3 0.0 copy-start
  1.3 0.0 copy-start.1
  1.3 87.0 %sweep.1.spr_ref = bf16[8,16,2,16,256]{4,3,2,1,0:T(8,128)(2,1)S(1)} custom-call(s32[8,2]{1,0:T(8,128)} %copy.7.offs_ref, f32[256,512]{1,0:T(8,128)} %bitcast.8, f32[256,512]{1,0:T(8,128)} %bitcast.9, bf16[8,2,256,256]{3,2,1,0:T(8,128)(2,1)} %exit_ref.1), custom_call_target="tpu_custom_call" | custom-call | tf_op jit(solution)/shard_map/sweep/pallas_call | solution.py:320
  88.3 0.0 copy-done
  88.4 0.0 copy-done.1
  88.4 2.1 %gather_other.2 = bf16[1,256,512]{2,1,0:T(8,128)(2,1)S(1)} custom-call(s32[8,2]{1,0:T(8,128)S(1)} %copy-done.1, bf16[8,2,256,256]{3,2,1,0:T(8,128)(2,1)S(1)} %bitcast.5, bf16[8,16,2,16,256]{4,3,2,1,0:T(8,128)(2,1)S(1)} %sweep.1.spr_ref), custom_call_target="tpu_custom_call" | custom-call | flops 20000000 | bytes 6000000 | tf_op jit(solution)/shard_map/gather_other/pallas_call | solution.py:415
  90.5 2.4 %collective-permute-start = (bf16[1,256,512]{2,1,0:T(8,128)(2,1)S(1)}, bf16[1,256,512]{2,1,0:T(8,128)(2,1)S(1)}, u32[]{:S(2)}, u32[]{:S(2)}) collective-permute-start(bf16[1,256,512]{2,1,0:T(8,128)(2,1)S(1)} %gather_other.2), channel_id=1, source_target_pairs={{0,1},{1,0},{2,3},{3,2},{4,5},{5,4},{6,7},{7,6},{8,9},{9,8},{10,11... | collective-permute-start | bytes 786440 | tf_op jit(solution)/shard_map/ppermute | solution.py:436
  92.9 2.1 %gather_other.3 = bf16[1,256,512]{2,1,0:T(8,128)(2,1)S(1)} custom-call(s32[8,2]{1,0:T(8,128)S(1)} %copy-done.1, bf16[8,2,256,256]{3,2,1,0:T(8,128)(2,1)S(1)} %bitcast.6, bf16[8,16,2,16,256]{4,3,2,1,0:T(8,128)(2,1)S(1)} %sweep.1.spr_ref), custom_call_target="tpu_custom_call" | custom-call | flops 20000000 | bytes 6000000 | tf_op jit(solution)/shard_map/gather_other/pallas_call | solution.py:415
  95.0 1.3 %collective-permute-start.1 = (bf16[1,256,512]{2,1,0:T(8,128)(2,1)S(1)}, bf16[1,256,512]{2,1,0:T(8,128)(2,1)S(1)}, u32[]{:S(2)}, u32[]{:S(2)}) collective-permute-start(bf16[1,256,512]{2,1,0:T(8,128)(2,1)S(1)} %gather_other.3), channel_id=1, source_target_pairs={{0,1},{1,0},{2,3},{3,2},{4,5},{5,4},{6,7},{7,6},{8,9},{9,8},{10,11... | collective-permute-start | bytes 786440 | tf_op jit(solution)/shard_map/ppermute | solution.py:436
  96.3 2.8 %gather_own.1 = f32[2,256,512]{2,1,0:T(8,128)S(1)} custom-call(s32[8,2]{1,0:T(8,128)S(1)} %copy-done.1, bf16[8,2,256,256]{3,2,1,0:T(8,128)(2,1)S(1)} %bitcast.7, bf16[8,16,2,16,256]{4,3,2,1,0:T(8,128)(2,1)S(1)} %sweep.1.spr_ref), custom_call_target="tpu_custom_call" | custom-call | flops 20000000 | bytes 6000000 | tf_op jit(solution)/shard_map/gather_own/pallas_call | solution.py:415
  99.1 2.0 %collective-permute-done = bf16[1,256,512]{2,1,0:T(8,128)(2,1)S(1)} collective-permute-done((bf16[1,256,512]{2,1,0:T(8,128)(2,1)S(1)}, bf16[1,256,512]{2,1,0:T(8,128)(2,1)S(1)}, u32[]{:S(2)}, u32[]{:S(2)}) %collective-permute-start) | collective-permute-done | bytes 262176 | tf_op jit(solution)/shard_map/ppermute | solution.py:436
  101.1 4.4 %collective-permute-done.1 = bf16[1,256,512]{2,1,0:T(8,128)(2,1)S(1)} collective-permute-done((bf16[1,256,512]{2,1,0:T(8,128)(2,1)S(1)}, bf16[1,256,512]{2,1,0:T(8,128)(2,1)S(1)}, u32[]{:S(2)}, u32[]{:S(2)}) %collective-permute-start.1) | collective-permute-done | bytes 262176 | tf_op jit(solution)/shard_map/ppermute | solution.py:436
  105.5 1.1 %add_bitcast_fusion = f32[1,2,256,512]{3,2,1,0:T(8,128)} fusion(f32[2,256,512]{2,1,0:T(8,128)S(1)} %gather_own.1, bf16[1,256,512]{2,1,0:T(8,128)(2,1)S(1)} %collective-permute-done.1, bf16[1,256,512]{2,1,0:T(8,128)(2,1)S(1)} %collective-permute-done), kind=kLoop, calls=%fused_computation | loop fusion | flops 786432 | bytes 2621440 | tf_op jit(solution)/shard_map/broadcast_in_dim | solution.py:439
Async XLA Ops:
  1.3 87.0 %copy-start = (bf16[1,8,2,256,256]{4,3,2,1,0:T(8,128)(2,1)S(1)}, bf16[1,8,2,256,256]{4,3,2,1,0:T(8,128)(2,1)}, u32[]{:S(2)}) copy-start(bf16[1,8,2,256,256]{4,3,2,1,0:T(8,128)(2,1)} %param.7) | copy-start | bytes 6291460
  1.3 87.0 %copy-start.1 = (s32[8,2]{1,0:T(8,128)S(1)}, s32[8,2]{1,0:T(8,128)}, u32[]{:S(2)}) copy-start(s32[8,2]{1,0:T(8,128)} %copy.7.offs_ref) | copy-start | bytes 196
  90.5 10.6 %collective-permute-start = (bf16[1,256,512]{2,1,0:T(8,128)(2,1)S(1)}, bf16[1,256,512]{2,1,0:T(8,128)(2,1)S(1)}, u32[]{:S(2)}, u32[]{:S(2)}) collective-permute-start(bf16[1,256,512]{2,1,0:T(8,128)(2,1)S(1)} %gather_other.2), channel_id=1, source_target_pairs={{0,1},{1,0},{2,3},{3,2},{4,5},{5,4},{6,7},{7,6},{8,9},{9,8},{10,11... | collective-permute-start | bytes 786440 | tf_op jit(solution)/shard_map/ppermute | solution.py:436
  95.0 10.5 %collective-permute-start.1 = (bf16[1,256,512]{2,1,0:T(8,128)(2,1)S(1)}, bf16[1,256,512]{2,1,0:T(8,128)(2,1)S(1)}, u32[]{:S(2)}, u32[]{:S(2)}) collective-permute-start(bf16[1,256,512]{2,1,0:T(8,128)(2,1)S(1)} %gather_other.3), channel_id=1, source_target_pairs={{0,1},{1,0},{2,3},{3,2},{4,5},{5,4},{6,7},{7,6},{8,9},{9,8},{10,11... | collective-permute-start | bytes 786440 | tf_op jit(solution)/shard_map/ppermute | solution.py:436

commit v10 on v9

--- a/solution.py
+++ b/solution.py
@@ -273,17 +273,19 @@
                 device_id_type=MESH,
             ).start()
 
-        for order in range(G):
-            lag = 2 * (order + 1)
-            for part in range(2):
-                for j in range(2):
-                    spread_out[before, order, part, :, 128 * j : 128 * j + 128] = tall[
-                        order, part, j, pl.ds(seen + lag, R), :
-                    ].astype(jnp.bfloat16)
-
-            @pl.when(jnp.logical_and(strip > 0, jnp.logical_and(group < LATE, member != G - 1 - order)))
-            def _():
-                send_spread(strip - 1, order)
+        @pl.when(strip > 0)
+        def _():
+            for order in range(G):
+                lag = 2 * (order + 1)
+                for part in range(2):
+                    for j in range(2):
+                        spread_out[before, order, part, :, 128 * j : 128 * j + 128] = tall[
+                            order, part, j, pl.ds(seen + lag, R), :
+                        ].astype(jnp.bfloat16)
+
+                @pl.when(jnp.logical_and(group < LATE, member != G - 1 - order))
+                def _():
+                    send_spread(strip - 1, order)
 
         @pl.when(strip > 0)
         def _():

time: 107 us -> 107 us (level)
  no operation moved by 1% of the time
where the time goes in v10:
time: 107 us
  Pallas kernels  93.9 us (88%)
  waiting for transfers between devices  6.21 us (6%)
  starting transfers between devices  4.01 us (4%)
  local copies, waits for them, and re-layouts  1.35 us (1%)
  other arithmetic  1.13 us (1%)
    pallas_call x1, Pallas kernels, sweep(): pl.pallas_call(sweep_kernel, out_shape=pltpu.VMEM((G, S - 1, 2, R, W), jn...  86.8 us
    pallas_call x3, Pallas kernels, gather(): pl.pallas_call(functools.partial(gather_kernel, other, parts), out_shape=...  7.07 us
    ppermute x2, waiting for transfers between devices, on_device(): lax.ppermute(gather(offsets, forward, spread, True, (part,)), 'scan', [(0...  6.21 us
    ppermute x2, starting transfers between devices, on_device(): lax.ppermute(gather(offsets, forward, spread, True, (part,)), 'scan', [(0...  4.01 us
  transfers between devices with their start and end apart: 2, of which 2 were waited for; matrix products, arithmetic and copies ran while one was open for 0% of the time, Pallas kernels for 5%

profile of v10, /device:TPU:0, one launch (start us, length us, event | category | flops | bytes accessed | tf_op | source)
XLA Modules:
  0.0 106.7 jit_solution(12321533494773808947)
XLA Ops:
  0.0 1.3 %copy.7.offs_ref = s32[8,2]{1,0:T(8,128)} copy(s32[8,2]{0,1:T(2,128)} %param.9) | data formatting | bytes 128 | tf_op args[4]
  1.3 0.0 copy-start
  1.3 0.0 copy-start.1
  1.3 86.8 %sweep.1.spr_ref = bf16[8,16,2,16,256]{4,3,2,1,0:T(8,128)(2,1)S(1)} custom-call(s32[8,2]{1,0:T(8,128)} %copy.7.offs_ref, f32[256,512]{1,0:T(8,128)} %bitcast.8, f32[256,512]{1,0:T(8,128)} %bitcast.9, bf16[8,2,256,256]{3,2,1,0:T(8,128)(2,1)} %exit_ref.1), custom_call_target="tpu_custom_call" | custom-call | tf_op jit(solution)/shard_map/sweep/pallas_call | solution.py:322
  88.2 0.0 copy-done
  88.2 0.0 copy-done.1
  88.2 2.0 %gather_other.2 = bf16[1,256,512]{2,1,0:T(8,128)(2,1)S(1)} custom-call(s32[8,2]{1,0:T(8,128)S(1)} %copy-done.1, bf16[8,2,256,256]{3,2,1,0:T(8,128)(2,1)S(1)} %bitcast.5, bf16[8,16,2,16,256]{4,3,2,1,0:T(8,128)(2,1)S(1)} %sweep.1.spr_ref), custom_call_target="tpu_custom_call" | custom-call | flops 20000000 | bytes 6000000 | tf_op jit(solution)/shard_map/gather_other/pallas_call | solution.py:417
  90.2 2.6 %collective-permute-start = (bf16[1,256,512]{2,1,0:T(8,128)(2,1)S(1)}, bf16[1,256,512]{2,1,0:T(8,128)(2,1)S(1)}, u32[]{:S(2)}, u32[]{:S(2)}) collective-permute-start(bf16[1,256,512]{2,1,0:T(8,128)(2,1)S(1)} %gather_other.2), channel_id=1, source_target_pairs={{0,1},{1,0},{2,3},{3,2},{4,5},{5,4},{6,7},{7,6},{8,9},{9,8},{10,11... | collective-permute-start | bytes 786440 | tf_op jit(solution)/shard_map/ppermute | solution.py:438
  92.9 2.0 %gather_other.3 = bf16[1,256,512]{2,1,0:T(8,128)(2,1)S(1)} custom-call(s32[8,2]{1,0:T(8,128)S(1)} %copy-done.1, bf16[8,2,256,256]{3,2,1,0:T(8,128)(2,1)S(1)} %bitcast.6, bf16[8,16,2,16,256]{4,3,2,1,0:T(8,128)(2,1)S(1)} %sweep.1.spr_ref), custom_call_target="tpu_custom_call" | custom-call | flops 20000000 | bytes 6000000 | tf_op jit(solution)/shard_map/gather_other/pallas_call | solution.py:417
  94.9 1.4 %collective-permute-start.1 = (bf16[1,256,512]{2,1,0:T(8,128)(2,1)S(1)}, bf16[1,256,512]{2,1,0:T(8,128)(2,1)S(1)}, u32[]{:S(2)}, u32[]{:S(2)}) collective-permute-start(bf16[1,256,512]{2,1,0:T(8,128)(2,1)S(1)} %gather_other.3), channel_id=1, source_target_pairs={{0,1},{1,0},{2,3},{3,2},{4,5},{5,4},{6,7},{7,6},{8,9},{9,8},{10,11... | collective-permute-start | bytes 786440 | tf_op jit(solution)/shard_map/ppermute | solution.py:438
  96.2 3.1 %gather_own.1 = f32[2,256,512]{2,1,0:T(8,128)S(1)} custom-call(s32[8,2]{1,0:T(8,128)S(1)} %copy-done.1, bf16[8,2,256,256]{3,2,1,0:T(8,128)(2,1)S(1)} %bitcast.7, bf16[8,16,2,16,256]{4,3,2,1,0:T(8,128)(2,1)S(1)} %sweep.1.spr_ref), custom_call_target="tpu_custom_call" | custom-call | flops 20000000 | bytes 6000000 | tf_op jit(solution)/shard_map/gather_own/pallas_call | solution.py:417
  99.3 1.7 %collective-permute-done = bf16[1,256,512]{2,1,0:T(8,128)(2,1)S(1)} collective-permute-done((bf16[1,256,512]{2,1,0:T(8,128)(2,1)S(1)}, bf16[1,256,512]{2,1,0:T(8,128)(2,1)S(1)}, u32[]{:S(2)}, u32[]{:S(2)}) %collective-permute-start) | collective-permute-done | bytes 262176 | tf_op jit(solution)/shard_map/ppermute | solution.py:438
  101.0 4.6 %collective-permute-done.1 = bf16[1,256,512]{2,1,0:T(8,128)(2,1)S(1)} collective-permute-done((bf16[1,256,512]{2,1,0:T(8,128)(2,1)S(1)}, bf16[1,256,512]{2,1,0:T(8,128)(2,1)S(1)}, u32[]{:S(2)}, u32[]{:S(2)}) %collective-permute-start.1) | collective-permute-done | bytes 262176 | tf_op jit(solution)/shard_map/ppermute | solution.py:438
  105.5 1.1 %add_bitcast_fusion = f32[1,2,256,512]{3,2,1,0:T(8,128)} fusion(f32[2,256,512]{2,1,0:T(8,128)S(1)} %gather_own.1, bf16[1,256,512]{2,1,0:T(8,128)(2,1)S(1)} %collective-permute-done.1, bf16[1,256,512]{2,1,0:T(8,128)(2,1)S(1)} %collective-permute-done), kind=kLoop, calls=%fused_computation | loop fusion | flops 786432 | bytes 2621440 | tf_op jit(solution)/shard_map/broadcast_in_dim | solution.py:441
Async XLA Ops:
  1.3 86.8 %copy-start = (bf16[1,8,2,256,256]{4,3,2,1,0:T(8,128)(2,1)S(1)}, bf16[1,8,2,256,256]{4,3,2,1,0:T(8,128)(2,1)}, u32[]{:S(2)}) copy-start(bf16[1,8,2,256,256]{4,3,2,1,0:T(8,128)(2,1)} %param.7) | copy-start | bytes 6291460
  1.3 86.9 %copy-start.1 = (s32[8,2]{1,0:T(8,128)S(1)}, s32[8,2]{1,0:T(8,128)}, u32[]{:S(2)}) copy-start(s32[8,2]{1,0:T(8,128)} %copy.7.offs_ref) | copy-start | bytes 196
  90.2 10.8 %collective-permute-start = (bf16[1,256,512]{2,1,0:T(8,128)(2,1)S(1)}, bf16[1,256,512]{2,1,0:T(8,128)(2,1)S(1)}, u32[]{:S(2)}, u32[]{:S(2)}) collective-permute-start(bf16[1,256,512]{2,1,0:T(8,128)(2,1)S(1)} %gather_other.2), channel_id=1, source_target_pairs={{0,1},{1,0},{2,3},{3,2},{4,5},{5,4},{6,7},{7,6},{8,9},{9,8},{10,11... | collective-permute-start | bytes 786440 | tf_op jit(solution)/shard_map/ppermute | solution.py:438
  94.9 10.7 %collective-permute-start.1 = (bf16[1,256,512]{2,1,0:T(8,128)(2,1)S(1)}, bf16[1,256,512]{2,1,0:T(8,128)(2,1)S(1)}, u32[]{:S(2)}, u32[]{:S(2)}) collective-permute-start(bf16[1,256,512]{2,1,0:T(8,128)(2,1)S(1)} %gather_other.3), channel_id=1, source_target_pairs={{0,1},{1,0},{2,3},{3,2},{4,5},{5,4},{6,7},{7,6},{8,9},{9,8},{10,11... | collective-permute-start | bytes 786440 | tf_op jit(solution)/shard_map/ppermute | solution.py:438
